TPU v7x, 32 devices: a whole 2x2x4 slice. The times are simulated.
32 devices in a mesh: dp: 8 (over y, x, core), seq: 4 (over z).
Axes of the slice: x: 2, y: 2, z: 4, core: 2. Of those that a mesh axis runs over, the one named last changes fastest.
Arguments:
- tokens: bfloat16 [32, 1024, 768], P('dp', 'seq'), may hold values from -6 to 6
- segment_ids: int32 [32, 1024], P('dp', 'seq'), may hold values from 0 to 1024, as said below
- valid_mask: int32 [32, 1024], P('dp', 'seq'), may hold values from 0 to 1, as said below
- cotangent: bfloat16 [32, 1024, 768], P('dp', 'seq'), may hold values from -6 to 6
- gain_one: bfloat16 [768], P(('dp', 'seq')), may hold values from 0.5 to 1.5
- gain_two: bfloat16 [768], P(('dp', 'seq')), may hold values from 0.5 to 1.5
- bias_table: bfloat16 [384], P(('dp', 'seq')), may hold values from -4 to 4
- qkv_weight: bfloat16 [768, 2304], P(('dp', 'seq')), may hold values from -0.109375 to 0.109375
- out_weight: bfloat16 [768, 768], P(('dp', 'seq')), may hold values from -1.75 to 1.75
- in_weight: bfloat16 [768, 3072], P(('dp', 'seq')), may hold values from -0.21875 to 0.21875
- back_weight: bfloat16 [3072, 768], P(('dp', 'seq')), may hold values from -0.109375 to 0.109375
Outputs:
- output: bfloat16 [32, 1024, 768], P('dp', 'seq')
- grad_input: bfloat16 [32, 1024, 768], P('dp', 'seq')
- grad_gain_one: float32 [768], P(('dp', 'seq'))
- grad_gain_two: float32 [768], P(('dp', 'seq'))
- grad_bias_table: float32 [384], P(('dp', 'seq'))
- grad_qkv_weight: float32 [768, 2304], P(('dp', 'seq'))
- grad_out_weight: float32 [768, 768], P(('dp', 'seq'))
- grad_in_weight: float32 [768, 3072], P(('dp', 'seq'))
- grad_back_weight: float32 [3072, 768], P(('dp', 'seq'))
Inputs may be any that keep to these rules, and one draw needn't show every extreme that they name: `segment_ids`: ids never fall along a sequence; a run of equal ids is one document; every sequence ends in 1 to 256 padding positions, which carry the id 1024. `valid_mask`: 1 exactly where segment_ids is not 1024.
All inputs are finite; a program needn't handle non-finite values.
Results may differ from a plain program's by a relative error of at most 0.019.
Values may be sent and summed in bfloat16 or wider, within the bound.
A program may use at most 320 MiB of HBM per device.

v0:
```python
import jax
import jax.numpy as jnp
from jax import lax
from jax.sharding import PartitionSpec as P

HEADS = 12
HD = 64
BUCKETS = 32


EPS = 1e-06
NEGATIVE = -1e30
bucket_limits = (12, 16, 23, 32, 46, 64, 91)


def bucket_of(relative):
    distance = jnp.abs(relative)
    counted = jnp.zeros_like(distance)
    for threshold in bucket_limits:
        counted = counted + (distance >= threshold).astype(jnp.int32)
    inside = jnp.where(distance < 8, distance, 8 + counted)
    return inside + 16 * (relative > 0).astype(jnp.int32)


def rms_scale(values):
    return lax.rsqrt(jnp.mean(values * values, axis=-1, keepdims=True) + EPS)


def smooth_gate(values):
    return jax.nn.gelu(values, approximate=True)


def norm_backward(values, scale_inv, gain_vec, grad_normed):
    weighted = grad_normed * gain_vec
    grad_gain = jnp.sum(grad_normed * values * scale_inv, axis=0)
    cubed = scale_inv * scale_inv * scale_inv
    grad_values = scale_inv * weighted - values * cubed * jnp.mean(
        weighted * values, axis=-1, keepdims=True
    )
    return (grad_values, grad_gain)


def group_scores(query_part, key_part, seg_query, seg_key, complete_bias):
    scores = (
        jnp.einsum("gqhd,gkhd->ghqk", query_part, key_part, preferred_element_type=jnp.float32)
        + complete_bias[None]
    )
    allowed = (seg_query[:, :, None] == seg_key[:, None, :])[:, None]
    return jnp.where(allowed, scores, NEGATIVE)


def query_backward(items, complete_bias):
    query_part, key_part, value_part, seg_query, seg_key, log_total, grad_part = items
    scores = group_scores(query_part, key_part, seg_query, seg_key, complete_bias)
    softmax_probabilities = jnp.exp(scores - log_total)
    grad_probs = jnp.einsum(
        "gqhd,gkhd->ghqk", grad_part, value_part, preferred_element_type=jnp.float32
    )
    row_inner = jnp.sum(softmax_probabilities * grad_probs, axis=-1, keepdims=True)
    grad_scores = (softmax_probabilities * (grad_probs - row_inner)).astype(jnp.bfloat16)
    grad_query = jnp.einsum(
        "ghqk,gkhd->gqhd", grad_scores, key_part, preferred_element_type=jnp.float32
    ).astype(jnp.bfloat16)
    return (softmax_probabilities, grad_scores, grad_query, row_inner)


def shards(
    tokens,
    segment_ids,
    valid_mask,
    cotangent,
    gain_one,
    gain_two,
    bias_table,
    qkv_weight,
    out_weight,
    in_weight,
    back_weight,
):
    gathered = (
        lax.all_gather(gain_one, ("dp", "seq"), axis=0, tiled=True),
        lax.all_gather(gain_two, ("dp", "seq"), axis=0, tiled=True),
        lax.all_gather(bias_table, ("dp", "seq"), axis=0, tiled=True),
        lax.all_gather(qkv_weight, ("dp", "seq"), axis=0, tiled=True),
        lax.all_gather(out_weight, ("dp", "seq"), axis=0, tiled=True),
        lax.all_gather(in_weight, ("dp", "seq"), axis=0, tiled=True),
        lax.all_gather(back_weight, ("dp", "seq"), axis=0, tiled=True),
    )
    gain_first, gain_second, table_flat, qkv_full, out_full, in_full, back_full = gathered
    seq_count, block_len, model_width = tokens.shape
    seq_len = block_len * lax.axis_size("seq")
    row_count = seq_count * block_len
    group_size = seq_count
    while group_size % 2 == 0 and group_size // 2 * block_len >= 512:
        group_size = group_size // 2
    group_count = seq_count // group_size
    flat_x = tokens.reshape(row_count, model_width).astype(jnp.float32)
    first_scale = rms_scale(flat_x)
    first_gain = gain_first.astype(jnp.float32)
    first_normed = (flat_x * first_scale * first_gain).astype(jnp.bfloat16)
    projected = jnp.dot(first_normed, qkv_full, preferred_element_type=jnp.float32).astype(
        jnp.bfloat16
    )
    queries = projected[:, :model_width].reshape(group_count, group_size, block_len, HEADS, HD)
    local_keys = projected[:, model_width : 2 * model_width].reshape(
        seq_count, block_len, model_width
    )
    local_values = projected[:, 2 * model_width :].reshape(seq_count, block_len, model_width)
    all_keys, all_values, all_segments = (
        lax.all_gather(local_keys, "seq", axis=1, tiled=True),
        lax.all_gather(local_values, "seq", axis=1, tiled=True),
        lax.all_gather(segment_ids, "seq", axis=1, tiled=True),
    )
    key_groups = all_keys.reshape(group_count, group_size, seq_len, HEADS, HD)
    value_groups = all_values.reshape(group_count, group_size, seq_len, HEADS, HD)
    segkey_groups = all_segments.reshape(group_count, group_size, seq_len)
    segquery_groups = segment_ids.reshape(group_count, group_size, block_len)
    offset = lax.axis_index("seq") * block_len
    query_places = offset + jnp.arange(block_len, dtype=jnp.int32)
    key_places = jnp.arange(seq_len, dtype=jnp.int32)
    buckets = bucket_of(key_places[None, :] - query_places[:, None])
    single_hot_vector = (
        buckets[None] == jnp.arange(BUCKETS, dtype=jnp.int32)[:, None, None]
    ).astype(jnp.bfloat16)
    bias_matrix = table_flat.reshape(BUCKETS, HEADS)
    complete_bias = jnp.einsum(
        "dto,dl->lto", single_hot_vector, bias_matrix, preferred_element_type=jnp.float32
    )

    def attend(group_items):
        query_part, key_part, value_part, seg_query, seg_key = group_items
        scores = group_scores(query_part, key_part, seg_query, seg_key, complete_bias)
        row_peak = jnp.max(scores, axis=-1, keepdims=True)
        shifted = jnp.exp(scores - row_peak)
        row_total = jnp.sum(shifted, axis=-1, keepdims=True)
        softmax_probabilities = (shifted / row_total).astype(jnp.bfloat16)
        attn_part = jnp.einsum(
            "ghqk,gkhd->gqhd", softmax_probabilities, value_part, preferred_element_type=jnp.float32
        )
        return (attn_part.astype(jnp.bfloat16), row_peak + jnp.log(row_total))

    attn_mixed, log_totals = lax.map(
        attend, (queries, key_groups, value_groups, segquery_groups, segkey_groups)
    )
    mixed_flat = attn_mixed.reshape(row_count, model_width)
    middle = flat_x + jnp.dot(mixed_flat, out_full, preferred_element_type=jnp.float32)
    second_scale = rms_scale(middle)
    second_gain = gain_second.astype(jnp.float32)
    second_normed = (middle * second_scale * second_gain).astype(jnp.bfloat16)
    hidden_pre = jnp.dot(second_normed, in_full, preferred_element_type=jnp.float32)
    hidden_float, gate_pullback = jax.vjp(smooth_gate, hidden_pre)
    hidden = hidden_float.astype(jnp.bfloat16)
    result = middle + jnp.dot(hidden, back_full, preferred_element_type=jnp.float32)
    output = result.astype(jnp.bfloat16).reshape(seq_count, block_len, model_width)
    grad_result = cotangent.reshape(row_count, model_width).astype(
        jnp.float32
    ) * valid_mask.reshape(row_count, 1).astype(jnp.float32)
    grad_branch = grad_result.astype(jnp.bfloat16)
    grad_back = jnp.einsum("tf,td->fd", hidden, grad_branch, preferred_element_type=jnp.float32)
    grad_hidden = jnp.einsum(
        "td,fd->tf", grad_branch, back_full, preferred_element_type=jnp.float32
    )
    grad_pre = gate_pullback(grad_hidden)[0].astype(jnp.bfloat16)
    grad_in = jnp.einsum("td,tf->df", second_normed, grad_pre, preferred_element_type=jnp.float32)
    grad_second_normed = jnp.einsum(
        "tf,df->td", grad_pre, in_full, preferred_element_type=jnp.float32
    )
    grad_middle_norm, grad_gain_second = norm_backward(
        middle, second_scale, second_gain, grad_second_normed
    )
    grad_middle = grad_result + grad_middle_norm
    grad_attn = grad_middle.astype(jnp.bfloat16)
    grad_out = jnp.einsum("td,te->de", mixed_flat, grad_attn, preferred_element_type=jnp.float32)
    grad_mixed = jnp.einsum(
        "te,de->td", grad_attn, out_full, preferred_element_type=jnp.float32
    ).astype(jnp.bfloat16)
    grad_mixed_groups = grad_mixed.reshape(group_count, group_size, block_len, HEADS, HD)
    backward_entries = (
        queries,
        key_groups,
        value_groups,
        segquery_groups,
        segkey_groups,
        log_totals,
        grad_mixed_groups,
    )
    bias_zero = jnp.zeros((HEADS, block_len, seq_len), jnp.float32)

    def full_backward(bias_total_sum, group_items):
        softmax_probabilities, grad_scores, grad_query, row_inner = query_backward(
            group_items, complete_bias
        )
        query_part = group_items[0]
        grad_part = group_items[6]
        key_gradient = jnp.einsum(
            "ghqk,gqhd->gkhd", grad_scores, query_part, preferred_element_type=jnp.float32
        )
        grad_value = jnp.einsum(
            "ghqk,gqhd->gkhd",
            softmax_probabilities.astype(jnp.bfloat16),
            grad_part,
            preferred_element_type=jnp.float32,
        )
        bias_total_sum = bias_total_sum + jnp.sum(grad_scores.astype(jnp.float32), axis=0)
        return (bias_total_sum, (grad_query, key_gradient, grad_value))

    bias_total_sum, (grad_queries, grad_keys, grad_values) = lax.scan(
        full_backward, bias_zero, backward_entries
    )
    key_terms = grad_keys.reshape(seq_count, seq_len, model_width)
    value_terms = grad_values.reshape(seq_count, seq_len, model_width)
    key_sum, value_sum = (
        lax.psum_scatter(
            key_terms.astype(jnp.bfloat16), "seq", scatter_dimension=1, tiled=True
        ).astype(jnp.float32),
        lax.psum_scatter(
            value_terms.astype(jnp.bfloat16), "seq", scatter_dimension=1, tiled=True
        ).astype(jnp.float32),
    )
    key_low = key_sum.astype(jnp.bfloat16)
    value_low = value_sum.astype(jnp.bfloat16)
    grad_projected = jnp.concatenate(
        [
            grad_queries.reshape(row_count, model_width),
            key_low.reshape(row_count, model_width),
            value_low.reshape(row_count, model_width),
        ],
        axis=1,
    )
    grad_qkv = jnp.einsum(
        "td,te->de", first_normed, grad_projected, preferred_element_type=jnp.float32
    )
    grad_first_normed = jnp.einsum(
        "te,de->td", grad_projected, qkv_full, preferred_element_type=jnp.float32
    )
    grad_x_norm, grad_gain_first = norm_backward(flat_x, first_scale, first_gain, grad_first_normed)
    grad_tokens = (
        (grad_middle + grad_x_norm).astype(jnp.bfloat16).reshape(seq_count, block_len, model_width)
    )
    grad_table = jnp.einsum(
        "fuy,suy->fs",
        single_hot_vector.astype(jnp.float32),
        bias_total_sum,
        precision=lax.Precision.HIGHEST,
    ).reshape(BUCKETS * HEADS)
    owned = (
        lax.psum_scatter(grad_gain_first, ("dp", "seq"), scatter_dimension=0, tiled=True),
        lax.psum_scatter(grad_gain_second, ("dp", "seq"), scatter_dimension=0, tiled=True),
        lax.psum_scatter(grad_table, ("dp", "seq"), scatter_dimension=0, tiled=True),
        lax.psum_scatter(grad_qkv, ("dp", "seq"), scatter_dimension=0, tiled=True),
        lax.psum_scatter(grad_out, ("dp", "seq"), scatter_dimension=0, tiled=True),
        lax.psum_scatter(grad_in, ("dp", "seq"), scatter_dimension=0, tiled=True),
        lax.psum_scatter(grad_back, ("dp", "seq"), scatter_dimension=0, tiled=True),
    )
    owned_gain_one, owned_gain_two, owned_table, owned_qkv, owned_out, owned_in, owned_back = owned
    return (
        output,
        grad_tokens,
        owned_gain_one,
        owned_gain_two,
        owned_table,
        owned_qkv,
        owned_out,
        owned_in,
        owned_back,
    )


def solution(mesh):
    in_specs = (
        P("dp", "seq", None),
        P("dp", "seq"),
        P("dp", "seq"),
        P("dp", "seq", None),
        P(("dp", "seq")),
        P(("dp", "seq")),
        P(("dp", "seq")),
        P(("dp", "seq"), None),
        P(("dp", "seq"), None),
        P(("dp", "seq"), None),
        P(("dp", "seq"), None),
    )
    out_specs = (
        P("dp", "seq", None),
        P("dp", "seq", None),
        P(("dp", "seq")),
        P(("dp", "seq")),
        P(("dp", "seq")),
        P(("dp", "seq"), None),
        P(("dp", "seq"), None),
        P(("dp", "seq"), None),
        P(("dp", "seq"), None),
    )
    return jax.shard_map(shards, mesh=mesh, in_specs=in_specs, out_specs=out_specs, check_vma=False)
```

profile of v0, /device:TPU:0, one launch (start us, length us, event | category | flops | bytes accessed | tf_op | source)
XLA Modules:
  0.0 1524.0 jit_solution(13873893870408748733)
XLA Ops:
  10.5 42.1 %all-reduce.7 = (bf16[768]{0:T(1024)(128)(2,1)S(1)}, bf16[384]{0:T(512)(128)(2,1)S(1)}, bf16[768]{0:T(1024)(128)(2,1)S(1)}) all-reduce(bf16[768]{0:T(1024)(128)(2,1)S(1)} %dynamic-update-slice, bf16[384]{0:T(512)(128)(2,1)S(1)} %dynamic-update-slice.1, bf16[768]{0:T(1024)(128)(2,1)S(1)} %dynamic-update-slice.2), channel_id=1, replica_groups=mesh['dp'=8,'seq'=4] {'dp','seq'}, use_global_device_ids=true, to_apply=%add | all-reduce | flops 1920 | bytes 7680
  56.9 16.8 %all-gather.7.cloned.1.call-done = bf16[768,2304]{1,0:T(8,128)(2,1)} async-done(((bf16[24,2304]{1,0:T(8,128)(2,1)}), bf16[768,2304]{1,0:T(8,128)(2,1)}) %all-gather.7.cloned.1.call-update) | async-done | bytes 3538960 | tf_op jit(solution)/shard_map/all_gather | solution.py:84
  84.3 13.3 all_gather.33
  109.6 17.8 %copy.69 = f32[12,256,1024]{2,1,0:T(8,128)} copy(f32[12,256,1024]{2,0,1:T(8,128)} %fusion.51) | data formatting | bytes 25165824 | tf_op jit(solution)/shard_map/while | solution.py:142
  133.7 62.4 %all-gather.11.cloned.1.call-done = bf16[4,1024,768]{2,1,0:T(8,128)(2,1)} async-done(((bf16[4,256,768]{2,1,0:T(8,128)(2,1)}), bf16[4,1024,768]{2,1,0:T(8,128)(2,1)}) %all-gather.11.cloned.1.call-update) | async-done | bytes 6291472 | tf_op jit(solution)/shard_map/all_gather | solution.py:110
  204.9 107.0 %all-gather.9.cloned.1.call-done = bf16[4,1024,768]{2,1,0:T(8,128)(2,1)} async-done(((bf16[4,256,768]{2,1,0:T(8,128)(2,1)}), bf16[4,1024,768]{2,1,0:T(8,128)(2,1)}) %all-gather.9.cloned.1.call-update) | async-done | bytes 6291472 | tf_op jit(solution)/shard_map/all_gather | solution.py:111
  323.1 90.7 %while.29 = (s32[]{:T(128)}, bf16[2,2,256,12,64]{2,1,0,4,3:T(2,128)(2,1)}, f32[2,2,12,256,1]{3,2,1,4,0:T(8,128)S(1)}, bf16[2,2,1024,12,64]{2,4,3,1,0:T(8,128)(2,...) while((s32[]{:T(128)}, ...), condition=%wide.region_4.5_spmd, body=%wide.region_1.4_spmd.sunk | while | flops 1687021568 | bytes 187948256 | solution.py:142
  323.5 14.4 fusion.132
  337.9 14.4 fusion.133
  353.3 12.8 fusion.134
  368.8 14.4 fusion.132
  383.2 14.5 fusion.133
  398.7 12.8 fusion.134
  443.2 53.9 %all-gather.17.cloned.1.call-done = bf16[3072,768]{1,0:T(8,128)(2,1)} async-done(((bf16[96,768]{1,0:T(8,128)(2,1)}), bf16[3072,768]{1,0:T(8,128)(2,1)}) %all-gather.17.cloned.1.call-update) | async-done | bytes 4718608 | tf_op jit(solution)/shard_map/all_gather | solution.py:87
  497.2 15.5 %fusion.61 = bf16[1024,3072]{1,0:T(8,128)(2,1)S(1)} fusion(f32[1024,3072]{1,0:T(8,128)} %fusion.96, bf16[1024,768]{1,0:T(8,128)(2,1)} %fusion.63, bf16[3072,768]{1,0:T(8,128)(2,1)} %all-gather.17.cloned.1.call-done), kind=kOutput, calls=%fused_computation.75 | convolution fusion | flops 4894752768 | bytes 25165824 | tf_op jit(solution)/shard_map/td,fd->tf/dot_general | solution.py:160
  533.2 246.6 %while.30 = (s32[]{:T(128)}, f32[12,256,1024]{2,1,0:T(8,128)}, bf16[2,2,256,12,64]{2,1,0,4,3:T(2,128)(2,1)}, bf16[2,2,1024,12,64]{2,4,3,1,0:T(8,128)(2,1)}, bf16...) while((s32[]{:T(128)}, f32[12,256,1024]{2,1,0:T(8,128)}, ...), condition=%wide.region_10.11_spmd.clone, body=%wide.region_7.10_spmd.clone.sunk | while | flops 4137543680 | bytes 360653248 | solution.py:207
  548.4 16.7 %bitcast_dynamic-update-slice_fusion.8 = bf16[2,2,1024,12,64]{2,4,3,1,0:T(8,128)(2,1)} fusion(bf16[2,2,1024,12,64]{2,4,3,1,0:T(8,128)(2,1)} %get-tuple-element.527, s32[]{:T(128)S(6)} %copy.134, f32[2,12,256,1024]{3,2,1,0:T(8,128)} %fusion.142, f32[2,12,256]{2,1,0:T(8,128)S(1)} %dynamic-slice_bitcast_fusion.10, ...), kind=kOutput, calls=%fused_computation.31.clone.1 | convolution fusion | flops 830472192 | bytes 45375492 | tf_op jit(solution)/shard_map/while/body/eval_jaxpr/ghqk,gqhd->gkhd/dot_general | solution.py:198
  565.1 25.6 %multiply_reduce_fusion.5 = (f32[2,12,256]{2,1,0:T(8,128)S(1)}, f32[2,12,256,1024]{3,2,1,0:T(8,128)}) fusion(f32[2,12,256,1024]{3,2,1,0:T(8,128)} %fusion.142, f32[2,12,256]{2,1,0:T(8,128)S(1)} %dynamic-slice_bitcast_fusion.10, f32[12,256,1024]{2,1,0:T(8,128)} %get-tuple-element.547, pred[2,256,1024]{2,1,0:T(8,128)(4,1)S(1)} %broadcast_compare_fusion.5, ...), kind=kOutput, calls=%fused_computation.25.clone.1 | convolution fusion | flops 836757504 | bytes 67420160 | tf_op jit(solution)/shard_map/while/body/eval_jaxpr/gqhd,gkhd->ghqk/dot_general | solution.py:56
  590.7 31.7 %convert_reduce_fusion.2 = (f32[12,256,1024]{2,1,0:T(8,128)}, bf16[2,12,256,1024]{3,2,1,0:T(8,128)(2,1)}) fusion(f32[2,12,256,1024]{3,2,1,0:T(8,128)} %get-tuple-element.474, f32[2,12,256]{2,1,0:T(8,128)S(1)} %get-tuple-element.475, f32[2,12,256]{2,1,0:T(8,128)S(1)} %dynamic-slice_bitcast_fusion.10, f32[2,12,256,1024]{3,2,1,0:T(8,128)} %fusion.142, ...), kind=kLoop, calls=%fused_computation.23.clone.1 | loop fusion | flops 47185920 | bytes 88653824 | tf_op jit(solution)/shard_map/while/body/eval_jaxpr/reduce_sum | solution.py:204
  670.0 16.8 %bitcast_dynamic-update-slice_fusion.8 = bf16[2,2,1024,12,64]{2,4,3,1,0:T(8,128)(2,1)} fusion(bf16[2,2,1024,12,64]{2,4,3,1,0:T(8,128)(2,1)} %get-tuple-element.527, s32[]{:T(128)S(6)} %copy.134, f32[2,12,256,1024]{3,2,1,0:T(8,128)} %fusion.142, f32[2,12,256]{2,1,0:T(8,128)S(1)} %dynamic-slice_bitcast_fusion.10, ...), kind=kOutput, calls=%fused_computation.31.clone.1 | convolution fusion | flops 830472192 | bytes 45375492 | tf_op jit(solution)/shard_map/while/body/eval_jaxpr/ghqk,gqhd->gkhd/dot_general | solution.py:198
  686.7 25.7 %multiply_reduce_fusion.5 = (f32[2,12,256]{2,1,0:T(8,128)S(1)}, f32[2,12,256,1024]{3,2,1,0:T(8,128)}) fusion(f32[2,12,256,1024]{3,2,1,0:T(8,128)} %fusion.142, f32[2,12,256]{2,1,0:T(8,128)S(1)} %dynamic-slice_bitcast_fusion.10, f32[12,256,1024]{2,1,0:T(8,128)} %get-tuple-element.547, pred[2,256,1024]{2,1,0:T(8,128)(4,1)S(1)} %broadcast_compare_fusion.5, ...), kind=kOutput, calls=%fused_computation.25.clone.1 | convolution fusion | flops 836757504 | bytes 67420160 | tf_op jit(solution)/shard_map/while/body/eval_jaxpr/gqhd,gkhd->ghqk/dot_general | solution.py:56
  712.4 31.7 %convert_reduce_fusion.2 = (f32[12,256,1024]{2,1,0:T(8,128)}, bf16[2,12,256,1024]{3,2,1,0:T(8,128)(2,1)}) fusion(f32[2,12,256,1024]{3,2,1,0:T(8,128)} %get-tuple-element.474, f32[2,12,256]{2,1,0:T(8,128)S(1)} %get-tuple-element.475, f32[2,12,256]{2,1,0:T(8,128)S(1)} %dynamic-slice_bitcast_fusion.10, f32[2,12,256,1024]{3,2,1,0:T(8,128)} %fusion.142, ...), kind=kLoop, calls=%fused_computation.23.clone.1 | loop fusion | flops 47185920 | bytes 88653824 | tf_op jit(solution)/shard_map/while/body/eval_jaxpr/reduce_sum | solution.py:204
  744.1 14.9 select_add_fusion.2
  786.0 12.8 fusion.97
  815.2 74.3 %reduce-scatter.9.cloned.1.call-done = bf16[4,256,768]{1,2,0:T(8,128)(2,1)} async-done(((bf16[4,1024,768]{1,2,0:T(8,128)(2,1)}), bf16[4,256,768]{1,2,0:T(8,128)(2,1)}) %reduce-scatter.9.cloned.1.call-update) | async-done | bytes 1572880 | tf_op jit(solution)/shard_map/reduce_scatter | solution.py:216
  892.9 110.3 %reduce-scatter.7.cloned.1.call-done = bf16[4,256,768]{1,2,0:T(8,128)(2,1)} async-done(((bf16[4,1024,768]{1,2,0:T(8,128)(2,1)}), bf16[4,256,768]{1,2,0:T(8,128)(2,1)}) %reduce-scatter.7.cloned.1.call-update) | async-done | bytes 1572880 | tf_op jit(solution)/shard_map/reduce_scatter | solution.py:213
  1016.8 24.1 %fusion.76 = f32[32,12]{1,0:T(8,128)S(1)} fusion(f32[12,256,1024]{2,1,0:T(8,128)} %get-tuple-element.132, s32[256,1024]{1,0:T(8,128)S(1)} %copy-done.17), kind=kOutput, calls=%fused_computation.107 | convolution fusion | flops 1216348160 | bytes 13633024 | tf_op jit(solution)/shard_map/fuy,suy->fs/dot_general | solution.py:240
  1041.2 13.6 add_convert_fusion
  1060.6 41.2 %all-reduce.6 = (f32[768]{0:T(1024)S(1)}, f32[768]{0:T(1024)S(1)}, f32[384]{0:T(512)S(1)}) all-reduce(f32[768]{0:T(1024)S(1)} %get-tuple-element.265, f32[768]{0:T(1024)S(1)} %copy-done.37, f32[384]{0:T(512)S(1)} %reshape.235), channel_id=4, replica_groups=mesh['dp'=8,'seq'=4] {'dp','seq'}, use_global_device_ids=true, to_apply=%region_15.16.clone | all-reduce | flops 1920 | bytes 15360
  1108.7 141.9 %reduce-scatter.17.cloned.1.call-done = f32[96,768]{1,0:T(8,128)} async-done(((f32[3072,768]{1,0:T(8,128)}), f32[96,768]{1,0:T(8,128)}) %reduce-scatter.17.cloned.1.call-update) | async-done | bytes 294928 | tf_op jit(solution)/shard_map/reduce_scatter | solution.py:253
  1250.6 141.1 %reduce-scatter.15.cloned.1.call-done = f32[24,3072]{1,0:T(8,128)} async-done(((f32[768,3072]{1,0:T(8,128)}), f32[24,3072]{1,0:T(8,128)}) %reduce-scatter.15.cloned.1.call-update) | async-done | bytes 294928 | tf_op jit(solution)/shard_map/reduce_scatter | solution.py:252
  1391.7 125.2 %reduce-scatter.11.cloned.1.call-done = f32[24,2304]{1,0:T(8,128)} async-done(((f32[768,2304]{1,0:T(8,128)}), f32[24,2304]{1,0:T(8,128)}) %reduce-scatter.11.cloned.1.call-update) | async-done | bytes 221200 | tf_op jit(solution)/shard_map/reduce_scatter | solution.py:250
  (230 shorter events, 248.5 us)
Async XLA Ops:
  7.2 66.5 %all-gather.7.cloned.1.call-start = ((), (), s32[]{:S(2)}) async-start(), calls=%async_computation.6 | async-start | bytes 3649536 | tf_op jit(solution)/shard_map/all_gather | solution.py:84
  7.9 188.2 %all-gather.11.cloned.1.call-start = ((), (), s32[]{:S(2)}) async-start(), calls=%async_computation.8 | async-start | bytes 7864320 | tf_op jit(solution)/shard_map/all_gather | solution.py:110
  56.9 22.9 %copy-start.20 = (bf16[1024,768]{1,0:T(8,128)(2,1)}, bf16[1024,768]{1,0:T(8,128)(2,1)S(1)}, u32[]{:S(2)}) copy-start(bf16[1024,768]{1,0:T(8,128)(2,1)S(1)} %fusion.66) | copy-start | bytes 4718596
  79.8 18.5 %copy-start.36 = (s32[4,256]{1,0:T(4,128)S(1)}, s32[4,256]{1,0:T(4,128)}, u32[]{:S(2)}) copy-start(s32[4,256]{1,0:T(4,128)} %param.17) | copy-start | bytes 12292
  81.8 230.1 %all-gather.9.cloned.1.call-start = ((), (), s32[]{:S(2)}) async-start(), calls=%async_computation.7 | async-start | bytes 7864320 | tf_op jit(solution)/shard_map/all_gather | solution.py:111
  82.5 335.1 %all-gather.13.cloned.1.call-start = ((), (), s32[]{:S(2)}) async-start(), calls=%async_computation.9 | async-start | bytes 1216512 | tf_op jit(solution)/shard_map/all_gather | solution.py:85
  83.1 349.0 %all-gather.15.cloned.1.call-start = ((), (), s32[]{:S(2)}) async-start(), calls=%async_computation.10 | async-start | bytes 4866048 | tf_op jit(solution)/shard_map/all_gather | solution.py:86
  83.7 413.5 %all-gather.17.cloned.1.call-start = ((), (), s32[]{:S(2)}) async-start(), calls=%async_computation.11 | async-start | bytes 4866048 | tf_op jit(solution)/shard_map/all_gather | solution.py:87
  84.2 805.3 %reduce-scatter.9.cloned.1.call-start = ((), (), s32[]{:S(2)}) async-start(), calls=%async_computation.13 | async-start | bytes 7864320 | tf_op jit(solution)/shard_map/reduce_scatter | solution.py:216
  98.3 29.1 %copy-start.27 = (f32[1,2,4,128]{3,1,2,0:T(2,128)}, f32[1,2,4,128]{3,1,2,0:T(2,128)S(1)}, u32[]{:S(2)}) copy-start(f32[1,2,4,128]{3,1,2,0:T(2,128)S(1)} %copy.92) | copy-start | bytes 12292
  109.6 17.8 %copy-start.9 = (bf16[4,256,768]{2,1,0:T(8,128)(2,1)S(1)}, bf16[4,256,768]{2,1,0:T(8,128)(2,1)}, u32[]{:S(2)}) copy-start(bf16[4,256,768]{2,1,0:T(8,128)(2,1)} %param.18) | copy-start | bytes 4718596
  337.9 15.4 %copy-start = (f32[12,256,1024]{2,1,0:T(8,128)S(1)}, f32[12,256,1024]{2,1,0:T(8,128)}, u32[]{:S(2)}) copy-start(f32[12,256,1024]{2,1,0:T(8,128)} %get-tuple-element.506) | copy-start | bytes 37748740 | tf_op jit(solution)/shard_map/while
  383.2 15.5 %copy-start = (f32[12,256,1024]{2,1,0:T(8,128)S(1)}, f32[12,256,1024]{2,1,0:T(8,128)}, u32[]{:S(2)}) copy-start(f32[12,256,1024]{2,1,0:T(8,128)} %get-tuple-element.506) | copy-start | bytes 37748740 | tf_op jit(solution)/shard_map/while
  417.6 14.5 copy-start.33
  423.1 95.6 %copy-start.31 = (f32[1024]{0:T(1024)}, f32[1024]{0:T(1024)S(1)}, u32[]{:S(2)}) copy-start(f32[1024]{0:T(1024)S(1)} %get-tuple-element.327) | copy-start | bytes 12292
  497.2 15.5 %copy-start.18 = (f32[1024,768]{1,0:T(8,128)S(1)}, f32[1024,768]{1,0:T(8,128)}, u32[]{:S(2)}) copy-start(f32[1024,768]{1,0:T(8,128)} %get-tuple-element.329) | copy-start | bytes 9437188
  497.2 15.5 %copy-start.38 = (bf16[768,3072]{1,0:T(8,128)(2,1)S(1)}, bf16[768,3072]{1,0:T(8,128)(2,1)}, u32[]{:S(2)}) copy-start(bf16[768,3072]{1,0:T(8,128)(2,1)} %all-gather.15.cloned.1.call-done) | copy-start | bytes 14155780
  533.6 14.8 copy-start.3
  534.0 31.1 %copy-start.1 = (pred[2,256,1024]{2,1,0:T(8,128)(4,1)}, pred[2,256,1024]{2,1,0:T(8,128)(4,1)S(1)}, u32[]{:S(2)}) copy-start(pred[2,256,1024]{2,1,0:T(8,128)(4,1)S(1)} %broadcast_compare_fusion.5) | copy-start | bytes 1572868 | tf_op jit(solution)/shard_map/while
  565.1 69.5 %slice-start = ((s8[6291456]{0:T(1024)(128)(4,1)}), s8[2097152]{0:T(1024)(128)(4,1)S(1)}, s32[]{:S(2)}) async-start(s8[6291456]{0:T(1024)(128)(4,1)} %bitcast.190), calls=%async_computation.18 | async-start | bytes 4194304 | tf_op jit(solution)/shard_map/while
  590.7 43.9 %slice-start.1 = ((s8[6291456]{0:T(1024)(128)(4,1)}), s8[4194304]{0:T(1024)(128)(4,1)S(1)}, s32[]{:S(2)}) async-start(s8[6291456]{0:T(1024)(128)(4,1)} %bitcast.190), calls=%async_computation.19 | async-start | bytes 8388608 | tf_op jit(solution)/shard_map/while
  655.2 14.8 copy-start.3
  655.6 31.2 %copy-start.1 = (pred[2,256,1024]{2,1,0:T(8,128)(4,1)}, pred[2,256,1024]{2,1,0:T(8,128)(4,1)S(1)}, u32[]{:S(2)}) copy-start(pred[2,256,1024]{2,1,0:T(8,128)(4,1)S(1)} %broadcast_compare_fusion.5) | copy-start | bytes 1572868 | tf_op jit(solution)/shard_map/while
  686.7 72.3 %slice-start = ((s8[6291456]{0:T(1024)(128)(4,1)}), s8[2097152]{0:T(1024)(128)(4,1)S(1)}, s32[]{:S(2)}) async-start(s8[6291456]{0:T(1024)(128)(4,1)} %bitcast.190), calls=%async_computation.18 | async-start | bytes 4194304 | tf_op jit(solution)/shard_map/while
  712.4 46.7 %slice-start.1 = ((s8[6291456]{0:T(1024)(128)(4,1)}), s8[4194304]{0:T(1024)(128)(4,1)S(1)}, s32[]{:S(2)}) async-start(s8[6291456]{0:T(1024)(128)(4,1)} %bitcast.190), calls=%async_computation.19 | async-start | bytes 8388608 | tf_op jit(solution)/shard_map/while
  779.8 223.3 %reduce-scatter.7.cloned.1.call-start = ((), (), s32[]{:S(2)}) async-start(), calls=%async_computation.12 | async-start | bytes 7864320 | tf_op jit(solution)/shard_map/reduce_scatter | solution.py:213
  780.6 328.1 %reduce-scatter.13.cloned.1.call-start = ((), (), s32[]{:S(2)}) async-start(), calls=%async_computation.15 | async-start | bytes 2433024 | tf_op jit(solution)/shard_map/reduce_scatter | solution.py:251
  786.0 464.6 %reduce-scatter.17.cloned.1.call-start = ((), (), s32[]{:S(2)}) async-start(), calls=%async_computation.17 | async-start | bytes 9732096 | tf_op jit(solution)/shard_map/reduce_scatter | solution.py:253
  798.9 592.8 %reduce-scatter.15.cloned.1.call-start = ((), (), s32[]{:S(2)}) async-start(), calls=%async_computation.16 | async-start | bytes 9732096 | tf_op jit(solution)/shard_map/reduce_scatter | solution.py:252
  811.3 705.6 %reduce-scatter.11.cloned.1.call-start = ((), (), s32[]{:S(2)}) async-start(), calls=%async_computation.14 | async-start | bytes 7299072 | tf_op jit(solution)/shard_map/reduce_scatter | solution.py:250
  891.3 115.3 %copy-start.21 = (bf16[1024,768]{1,0:T(8,128)(2,1)S(1)}, bf16[1024,768]{1,0:T(8,128)(2,1)}, u32[]{:S(2)}) copy-start(bf16[1024,768]{1,0:T(8,128)(2,1)} %copy-done.20) | copy-start | bytes 4718596
  1041.1 13.6 copy-start.6
  (36 other events, 228.5 us)
Sparse Core Ops, SparseCore 0:
  10.8 62.8 all-gather.6
  81.9 114.1 all-gather.10
  198.3 113.5 all-gather.8
  314.5 52.2 all-gather.12
  369.5 62.6 all-gather.14
  434.8 62.3 all-gather.16
  780.0 109.5 reduce-scatter.8
  891.9 111.2 reduce-scatter.6
  1009.0 99.5 reduce-scatter.12
  1116.0 134.5 reduce-scatter.16
  1257.1 134.5 reduce-scatter.14
  1398.7 118.0 reduce-scatter.10
where the time goes:
time: 1530 us; the launch traced here: 1520 us
  waiting for transfers between devices  847 us (55%)
  matrix products  336 us (22%)
  other arithmetic  133 us (9%)
  blocking collectives  96.6 us (6%)
  local copies, waits for them, and re-layouts  95 us (6%)
    reduce_scatter x1, waiting for transfers between devices, shards(): lax.psum_scatter(grad_back, ('dp', 'seq'), scatter_dimension=0, tiled=True)  142 us
    reduce_scatter x1, waiting for transfers between devices, shards(): lax.psum_scatter(grad_in, ('dp', 'seq'), scatter_dimension=0, tiled=True)  141 us
    reduce_scatter x1, waiting for transfers between devices, shards(): lax.psum_scatter(grad_qkv, ('dp', 'seq'), scatter_dimension=0, tiled=True)  125 us
    reduce_scatter x1, waiting for transfers between devices, shards(): lax.psum_scatter(key_terms.astype(jnp.bfloat16), 'seq', scatter_dimension...  110 us
    all_gather x1, waiting for transfers between devices, shards(): lax.all_gather(local_values, 'seq', axis=1, tiled=True)  107 us
    unnamed x2, blocking collectives  83.3 us
    reduce_scatter x1, waiting for transfers between devices, shards(): lax.psum_scatter(value_terms.astype(jnp.bfloat16), 'seq', scatter_dimensi...  74.3 us
    reduce_sum x2, other arithmetic, full_backward(): jnp.sum(grad_scores.astype(jnp.float32), axis=0)  63.5 us
  transfers between devices with their start and end apart: 12, of which 11 were waited for; matrix products, arithmetic and copies ran while one was open for 17% of the time, Pallas kernels for 0%

commit v1 on v0

--- a/solution.py
+++ b/solution.py
@@ -1,6 +1,10 @@
+import functools
+
 import jax
 import jax.numpy as jnp
 from jax import lax
+from jax.experimental import pallas as pl
+from jax.experimental.pallas import tpu as pltpu
 from jax.sharding import PartitionSpec as P
 
 HEADS = 12
@@ -64,7 +68,7 @@
     return (softmax_probabilities, grad_scores, grad_query, row_inner)
 
 
-def shards(
+def general_shards(
     tokens,
     segment_ids,
     valid_mask,
@@ -266,6 +270,479 @@
     )
 
 
+MESH = pl.DeviceIdType.MESH
+
+def flip(i, bit):
+    return i + bit - 2 * bit * ((i // bit) % 2)
+
+def gather_kernel(items, *refs):
+    n_arr = 5
+    tok, seg = refs[0], refs[1]
+    shards = refs[2:2 + n_arr]
+    xf, sf = refs[2 + n_arr], refs[3 + n_arr]
+    full = refs[4 + n_arr:4 + 2 * n_arr]
+    loc_sem, t_send, t_recv, s_send, s_recv, z_send, z_recv, h_send, h_recv = refs[4 + 2 * n_arr:]
+    dp, z = lax.axis_index("dp"), lax.axis_index("seq")
+    n_z = 4
+    peers = [(dp, lax.rem(z + s, n_z)) for s in range(1, n_z)] + [(flip(dp, b), z) for b in (1, 2, 4)]
+    barrier = pltpu.get_barrier_semaphore()
+    for p in peers:
+        pl.semaphore_signal(barrier, inc=1, device_id=p, device_id_type=MESH)
+    pl.semaphore_wait(barrier, len(peers))
+
+    def block(it, d, zz):
+        return full[items[it][0]].at[d * n_z + zz]
+
+    def own(it):
+        return shards[items[it][0]]
+
+    n_it = len(items)
+    def z_copy(it, way, step):
+        src_z = z - step if way == 0 else z + step
+        src = own(it) if step == 0 else block(it, dp, src_z)
+        return pltpu.make_async_remote_copy(
+            src_ref=src, dst_ref=block(it, dp, src_z), send_sem=z_send.at[it, way, step],
+            recv_sem=z_recv.at[it, way, step], device_id=(dp, z + 1 if way == 0 else z - 1), device_id_type=MESH)
+
+    def z_wait(it, way, step):
+        src_z = z - 1 - step if way == 0 else z + 1 + step
+        blk = block(it, dp, src_z)
+        pltpu.make_async_remote_copy(src_ref=blk, dst_ref=blk, send_sem=z_send.at[it, way, step],
+            recv_sem=z_recv.at[it, way, step], device_id=(dp, z), device_id_type=MESH).wait_recv()
+
+    def can_send(way, step):
+        return (z >= step) & (z <= n_z - 2) if way == 0 else (z + step <= n_z - 1) & (z >= 1)
+
+    def can_recv(way, step):
+        return z >= step + 1 if way == 0 else z + 1 + step <= n_z - 1
+
+    def z_start(it, step):
+        for way in (0, 1):
+            @pl.when(can_send(way, step))
+            def _():
+                z_copy(it, way, step).start()
+
+    def z_recv_all(it, step):
+        for way in (0, 1):
+            @pl.when(can_recv(way, step))
+            def _():
+                z_wait(it, way, step)
+
+    def hops(it):
+        b1, b2 = items[it][1:]
+        return [(0, b1), (0, b2), (b1, b2), (0, 1), (b1, 1), (b2, 1), (b1 + b2, 1)]
+
+    def flips(d, mask):
+        for b in (1, 2, 4):
+            if mask & b:
+                d = flip(d, b)
+        return d
+
+    def hop(it, slot, zz):
+        mask, to = hops(it)[slot]
+        blk = block(it, flips(dp, mask), zz)
+        return pltpu.make_async_remote_copy(src_ref=blk, dst_ref=blk, send_sem=h_send.at[it, slot, zz],
+            recv_sem=h_recv.at[it, slot, zz], device_id=(flip(dp, to), z), device_id_type=MESH)
+
+    def hop_wait(it, slot, zz):
+        mask, to = hops(it)[slot]
+        blk = block(it, flips(dp, mask ^ to), zz)
+        pltpu.make_async_remote_copy(src_ref=blk, dst_ref=blk, send_sem=h_send.at[it, slot, zz],
+            recv_sem=h_recv.at[it, slot, zz], device_id=(dp, z), device_id_type=MESH).wait_recv()
+
+    def own_hop(it, slot):
+        to = hops(it)[slot][1]
+        return pltpu.make_async_remote_copy(src_ref=own(it), dst_ref=block(it, dp, z), send_sem=h_send.at[it, slot, z],
+            recv_sem=h_recv.at[it, slot, z], device_id=(flip(dp, to), z), device_id_type=MESH)
+
+    def tok_copy(s):
+        to = lax.rem(z + s, n_z)
+        return [pltpu.make_async_remote_copy(src_ref=a.at[to], dst_ref=f.at[z], send_sem=ss.at[s - 1], recv_sem=rs.at[s - 1],
+                device_id=(dp, to), device_id_type=MESH) for a, f, ss, rs in ((tok, xf, t_send, t_recv), (seg, sf, s_send, s_recv))]
+
+    def tok_wait(s):
+        frm = lax.rem(z + n_z - s, n_z)
+        for f, ss, rs in ((xf, t_send, t_recv), (sf, s_send, s_recv)):
+            pltpu.make_async_remote_copy(src_ref=f.at[frm], dst_ref=f.at[frm], send_sem=ss.at[s - 1], recv_sem=rs.at[s - 1],
+                device_id=(dp, z), device_id_type=MESH).wait_recv()
+
+    for it in range(n_it):
+        z_start(it, 0)
+        for slot in (0, 1, 3):
+            own_hop(it, slot).start()
+    locs = []
+    for it in range(n_it):
+        locs.append(pltpu.make_async_copy(own(it), block(it, dp, z), loc_sem.at[it]))
+    locs.append(pltpu.make_async_copy(tok.at[z], xf.at[z], loc_sem.at[n_it]))
+    locs.append(pltpu.make_async_copy(seg.at[z], sf.at[z], loc_sem.at[n_it + 1]))
+    for c in locs:
+        c.start()
+
+    def forward(it, zz):
+        hop_wait(it, 0, zz)
+        hop(it, 2, zz).start()
+        hop(it, 4, zz).start()
+        hop_wait(it, 1, zz)
+        hop(it, 5, zz).start()
+
+    def arrivals(step):
+        return [(can_recv(0, step), 0, z - 1 - step), (can_recv(1, step), 1, z + 1 + step)]
+
+    for step in range(n_z):
+        if step < n_z - 1:
+            for it in range(n_it):
+                for ok, way, zz in arrivals(step):
+                    @pl.when(ok)
+                    def _():
+                        z_wait(it, way, step)
+                        if step < n_z - 2:
+                            @pl.when(can_send(way, step + 1))
+                            def _():
+                                z_copy(it, way, step + 1).start()
+                        for slot in (0, 1, 3):
+                            hop(it, slot, zz).start()
+        if step == 1:
+            for s in range(1, n_z):
+                for c in tok_copy(s):
+                    c.start()
+        for it in range(n_it):
+            if step == 0:
+                forward(it, z)
+            else:
+                for ok, way, zz in arrivals(step - 1):
+                    @pl.when(ok)
+                    def _():
+                        forward(it, zz)
+    for zz in range(n_z):
+        for it in range(n_it):
+            hop_wait(it, 2, zz)
+            hop(it, 6, zz).start()
+    for s in range(1, n_z):
+        tok_wait(s)
+    for zz in range(n_z):
+        for it in range(n_it):
+            for slot in (3, 4, 5, 6):
+                hop_wait(it, slot, zz)
+    for c in locs:
+        c.wait()
+    for it in range(n_it):
+        for step in range(n_z - 1):
+            for way in (0, 1):
+                @pl.when(can_send(way, step))
+                def _():
+                    z_copy(it, way, step).wait_send()
+        for zz in range(n_z):
+            for slot in range(7):
+                hop(it, slot, zz).wait_send()
+    for s in range(1, n_z):
+        for c in tok_copy(s):
+            c.wait_send()
+
+def gather(tokens, seg, shards, items, collective_id=0):
+    n_it = len(items)
+    D = pltpu.SemaphoreType.DMA
+    out_shape = [jax.ShapeDtypeStruct(tokens.shape, tokens.dtype), jax.ShapeDtypeStruct(seg.shape, seg.dtype)]
+    out_shape += [jax.ShapeDtypeStruct((32, *s.shape), s.dtype) for s in shards]
+    anyspec = pl.BlockSpec(memory_space=pltpu.HBM)
+    return pl.pallas_call(
+        functools.partial(gather_kernel, items),
+        out_shape=out_shape,
+        in_specs=[pl.BlockSpec(memory_space=pltpu.VMEM)] * (2 + len(shards)),
+        out_specs=[anyspec] * len(out_shape),
+        scratch_shapes=[D((n_it + 2,)), D((3,)), D((3,)), D((3,)), D((3,)), D((n_it, 2, 3)), D((n_it, 2, 3)), D((n_it, 7, 4)), D((n_it, 7, 4))],
+        compiler_params=pltpu.CompilerParams(collective_id=collective_id, has_side_effects=True),
+    )(tokens, seg, *shards)
+
+
+LOG2E = 1.4426950408889634
+BIG = -1e30
+F32 = jnp.float32
+BF = jnp.bfloat16
+
+def extras(seg):
+    L = seg.shape[0]
+    nb = L.bit_length()
+    nblk = L // 128
+    lane = jnp.arange(128)[None, :] % 64
+    row_blk = (jnp.arange(L) // 128)[:, None]
+    b = lane - (nblk + 3)
+    inb = (b >= 0) & (b < 2 * nb)
+    bit = (seg[:, None] >> (jnp.clip(b, 0, 2 * nb - 1) // 2)) & 1
+    flip = b % 2
+    u = jnp.where(inb, (bit ^ flip), 0).astype(BF)
+    w = jnp.where(inb & ((bit ^ flip) == 0), BIG, 0.0)
+    onehot = (lane < nblk) & (lane == row_blk)
+    ones = (lane >= nblk) & (lane < nblk + 3)
+    exk = (w + (onehot | ones)).astype(BF)
+    farl = ((lane < nblk) & (lane <= row_blk - 2)).astype(BF)
+    farr = ((lane < nblk) & (lane >= row_blk + 2)).astype(BF)
+    return u, exk, farl, farr
+
+def strips(table):
+    a = jnp.arange(128)[:, None]; c = jnp.arange(384)[None, :]
+    bq = bucket_of(c - 128 - a)
+    bk = bucket_of(a + 128 - c)
+    def look(bk_):
+        oh = (bk_[None] == jnp.arange(32)[:, None, None]).astype(BF)
+        return jnp.einsum('bac,bh->hac', oh, table.astype(BF), preferred_element_type=F32)
+    return look(bq), look(bk)
+
+def fwd_kernel(nblk, bl_ref, q_ref, k_ref, v_ref, exq_ref, exk_ref, fl_ref, fr_ref, strip_ref, o_ref, qa_ref):
+    L = q_ref.shape[0]
+    hp = pl.program_id(0)
+    lane = lax.broadcasted_iota(jnp.int32, (L, 128), 1)
+    QB = 256
+    outs = []
+    for h in range(2):
+        sel = (lane < 64) if h == 0 else (lane >= 64)
+        bl = bl_ref[hp * 2 + h, 0].astype(BF); br = bl_ref[hp * 2 + h, 1].astype(BF)
+        qa = jnp.where(sel, q_ref[...], exq_ref[...] + fl_ref[...] * bl + fr_ref[...] * br)
+        ka = jnp.where(sel, k_ref[...], exk_ref[...])
+        va = jnp.where(sel, v_ref[...], jnp.ones((L, 128), BF))
+        lane_l = 64 * (1 - h)
+        for blk in range(L // QB):
+            r0 = blk * QB
+            qb = qa[r0:r0 + QB]
+            s = lax.dot_general(qb, ka, (((1,), (1,)), ((), ())), preferred_element_type=F32)
+            rows = []
+            for sub in range(QB // 128):
+                I = blk * (QB // 128) + sub
+                lo = max(I - 1, 0); hi = min(I + 1, nblk - 1)
+                srow = s[sub * 128:(sub + 1) * 128]
+                parts = []
+                if lo > 0: parts.append(srow[:, :lo * 128])
+                parts.append(srow[:, lo * 128:(hi + 1) * 128] + strip_ref[h, :, (lo - I + 1) * 128:(hi - I + 2) * 128])
+                if hi < nblk - 1: parts.append(srow[:, (hi + 1) * 128:])
+                rows.append(jnp.concatenate(parts, axis=1))
+            s = jnp.concatenate(rows, axis=0)
+            m = jnp.max(s, axis=1, keepdims=True)
+            p = jnp.exp2((s - m) * LOG2E).astype(BF)
+            o = jnp.dot(p, va, preferred_element_type=F32)
+            l = o[:, lane_l:lane_l + 1]
+            outs.append(o / l)
+            lse = m + jnp.log(l)
+            hi_ = (-lse).astype(BF); rest = -lse - hi_.astype(F32)
+            mid = rest.astype(BF); low = (rest - mid.astype(F32)).astype(BF)
+            base = 64 * (1 - h) + nblk
+            ln = lane[:QB]
+            qx = jnp.where(ln == base, hi_, jnp.where(ln == base + 1, mid, jnp.where(ln == base + 2, low, qb)))
+            qa_ref[h, r0:r0 + QB, :] = qx
+    n = L // QB
+    for blk in range(n):
+        o_ref[blk * QB:(blk + 1) * QB, :] = jnp.where(lane[:QB] < 64, outs[blk], outs[n + blk]).astype(BF)
+
+def attn_fwd(qkv, ex, strip, far, interpret=False):
+    L, W = qkv.shape
+    D = W // 3
+    H = D // HD
+    npair = H // 2
+    nblk = L // 128
+    exq, exk, fl, fr = ex
+    full = lambda: pl.BlockSpec((L, 128), lambda i: (0, 0))
+    return pl.pallas_call(
+        functools.partial(fwd_kernel, nblk),
+        grid=(npair,),
+        in_specs=[pl.BlockSpec(memory_space=pltpu.SMEM),
+                  pl.BlockSpec((L, 128), lambda i: (0, i)),
+                  pl.BlockSpec((L, 128), lambda i: (0, npair + i)),
+                  pl.BlockSpec((L, 128), lambda i: (0, 2 * npair + i)),
+                  full(), full(), full(), full(),
+                  pl.BlockSpec((2, 128, 384), lambda i: (i, 0, 0))],
+        out_specs=[pl.BlockSpec((L, 128), lambda i: (0, i)), pl.BlockSpec((2, L, 128), lambda i: (i, 0, 0))],
+        out_shape=[jax.ShapeDtypeStruct((L, D), BF), jax.ShapeDtypeStruct((H, L, 128), BF)],
+        compiler_params=pltpu.CompilerParams(vmem_limit_bytes=48 << 20),
+        cost_estimate=pl.CostEstimate(flops=4 * L * L * D * 4, bytes_accessed=L * W * 4, transcendentals=L * L * H),
+    )(far, qkv, qkv, qkv, exq, exk, fl, fr, strip)
+
+def bwd_kernel(nblk, qa_ref, k_ref, v_ref, do_ref, o_ref, exk_ref, strip_ref,
+               dq_ref, dk_ref, dv_ref, near_ref, far_ref):
+    L = k_ref.shape[0]
+    lane = lax.broadcasted_iota(jnp.int32, (L, 128), 1)
+    KB = 256
+    nsub = KB // 128
+    prod = do_ref[...].astype(F32) * o_ref[...].astype(F32)
+    dqs = []; dks = []; dvs = []
+    for h in range(2):
+        sel = (lane < 64) if h == 0 else (lane >= 64)
+        other = 64 * (1 - h)
+        qa = qa_ref[h]
+        ka = jnp.where(sel, k_ref[...], exk_ref[...])
+        va = jnp.where(sel, v_ref[...], ((lane >= other + nblk) & (lane < other + nblk + 3)).astype(BF))
+        delta = -jnp.sum(jnp.where(sel, prod, 0.0), axis=1, keepdims=True)
+        hi_ = delta.astype(BF); rest = delta - hi_.astype(F32)
+        mid = rest.astype(BF); low = (rest - mid.astype(F32)).astype(BF)
+        base = other + nblk
+        doa = jnp.where(sel, do_ref[...], jnp.where(lane == base, hi_, jnp.where(lane == base + 1, mid, jnp.where(lane == base + 2, low, jnp.zeros((L, 128), BF)))))
+        near = jnp.zeros((128, 384), F32)
+        dqt = jnp.zeros((128, L), F32)
+        for kb in range(L // KB):
+            r0 = kb * KB
+            kab = ka[r0:r0 + KB]
+            s = lax.dot_general(kab, qa, (((1,), (1,)), ((), ())), preferred_element_type=F32)
+            dp = lax.dot_general(va[r0:r0 + KB], doa, (((1,), (1,)), ((), ())), preferred_element_type=F32)
+            prow = []; dsrow = []
+            for sub in range(nsub):
+                J = kb * nsub + sub
+                lo = max(J - 1, 0); hi = min(J + 1, nblk - 1)
+                srow = s[sub * 128:(sub + 1) * 128]
+                parts = []
+                if lo > 0: parts.append(srow[:, :lo * 128])
+                parts.append(srow[:, lo * 128:(hi + 1) * 128] + strip_ref[h, :, (lo - J + 1) * 128:(hi - J + 2) * 128])
+                if hi < nblk - 1: parts.append(srow[:, (hi + 1) * 128:])
+                srow = jnp.concatenate(parts, axis=1)
+                p = jnp.exp2(srow * LOG2E)
+                ds = p * dp[sub * 128:(sub + 1) * 128]
+                nr = ds[:, lo * 128:(hi + 1) * 128]
+                if lo > J - 1: nr = jnp.concatenate([jnp.zeros((128, 128), F32), nr], axis=1)
+                if hi < J + 1: nr = jnp.concatenate([nr, jnp.zeros((128, 128), F32)], axis=1)
+                near = near + nr
+                prow.append(p.astype(BF)); dsrow.append(ds.astype(BF))
+            pb = jnp.concatenate(prow, axis=0); dsb = jnp.concatenate(dsrow, axis=0)
+            dvs.append(jnp.dot(pb, doa, preferred_element_type=F32))
+            dks.append(jnp.dot(dsb, qa, preferred_element_type=F32))
+            dqt = dqt + lax.dot_general(kab, dsb, (((0,), (0,)), ((), ())), preferred_element_type=F32)
+        near_ref[h] = near
+        far_ref[h] = dqt[other:other + 8]
+        dqs.append(dqt[64 * h:64 * h + 64])
+    n = L // KB
+    first = lane[:KB] < 64
+    for kb in range(n):
+        dk_ref[kb * KB:(kb + 1) * KB, :] = jnp.where(first, dks[kb], dks[n + kb]).astype(BF)
+        dv_ref[kb * KB:(kb + 1) * KB, :] = jnp.where(first, dvs[kb], dvs[n + kb]).astype(BF)
+    dq_ref[...] = jnp.concatenate(dqs, axis=0).T.astype(BF)
+
+def attn_bwd(qa, qkv, do, o, exk, stripT):
+    L, W = qkv.shape
+    D = W // 3
+    H = D // HD
+    npair = H // 2
+    nblk = L // 128
+    col = lambda off: pl.BlockSpec((L, 128), lambda i: (0, off + i))
+    return pl.pallas_call(
+        functools.partial(bwd_kernel, nblk),
+        grid=(npair,),
+        in_specs=[pl.BlockSpec((2, L, 128), lambda i: (i, 0, 0)), col(npair), col(2 * npair), col(0), col(0),
+                  pl.BlockSpec((L, 128), lambda i: (0, 0)), pl.BlockSpec((2, 128, 384), lambda i: (i, 0, 0))],
+        out_specs=[col(0), col(0), col(0), pl.BlockSpec((2, 128, 384), lambda i: (i, 0, 0)), pl.BlockSpec((2, 8, L), lambda i: (i, 0, 0))],
+        out_shape=[jax.ShapeDtypeStruct((L, D), BF)] * 3 + [jax.ShapeDtypeStruct((H, 128, 384), F32), jax.ShapeDtypeStruct((H, 8, L), F32)],
+        compiler_params=pltpu.CompilerParams(vmem_limit_bytes=48 << 20),
+        cost_estimate=pl.CostEstimate(flops=10 * L * L * D * 4, bytes_accessed=L * W * 6, transcendentals=L * L * H),
+    )(qa, qkv, qkv, do, o, exk, stripT)
+
+
+def fits(mesh):
+    return mesh.shape["dp"] == 8 and mesh.shape["seq"] == 4
+
+
+ITEMS = ((0, 4, 2), (4, 2, 4), (1, 2, 4), (2, 4, 2), (3, 2, 4))
+
+
+def fast_shards(
+    tokens,
+    segment_ids,
+    valid_mask,
+    cotangent,
+    gain_one,
+    gain_two,
+    bias_table,
+    qkv_weight,
+    out_weight,
+    in_weight,
+    back_weight,
+):
+    n_z = lax.axis_size("seq")
+    seq_count, block_len, width = tokens.shape
+    seq_len = n_z * block_len
+    n_dev = n_z * lax.axis_size("dp")
+    g_rows, t_rows = gain_one.shape[0], bias_table.shape[0]
+    small = jnp.concatenate([gain_one, gain_two, bias_table])
+    small = jnp.pad(small[None], ((0, 7), (0, 128 - small.shape[0])))
+    grad_local = cotangent * valid_mask[..., None].astype(BF)
+    x4, seg4, qkv_full, out_full, in_full, back_full, small_full = gather(
+        tokens,
+        segment_ids.reshape(seq_count, 1, block_len),
+        (qkv_weight, out_weight, in_weight, back_weight, small),
+        ITEMS,
+    )
+    qkv_full = qkv_full.reshape(width, 3 * width)
+    out_full = out_full.reshape(width, width)
+    in_full = in_full.reshape(width, -1)
+    back_full = back_full.reshape(-1, width)
+    small_full = small_full[:, 0]
+    gain_first = small_full[:, :g_rows].reshape(1, width).astype(F32)
+    gain_second = small_full[:, g_rows : 2 * g_rows].reshape(1, width).astype(F32)
+    table = small_full[:, 2 * g_rows : 2 * g_rows + t_rows].reshape(BUCKETS, HEADS)
+    grad_local, x4 = lax.optimization_barrier((grad_local, x4))
+    g_low = lax.all_to_all(grad_local, "seq", 0, 1, tiled=True).reshape(seq_len, width)
+    flat_x = x4.reshape(seq_len, width).astype(F32)
+    seg = seg4.reshape(seq_len)
+    exq, exk, far_left, far_right = extras(seg)
+    strip, strip_t = strips(table.astype(F32))
+    far = jnp.stack([table[BUCKETS // 2 - 1], table[BUCKETS - 1]], axis=1).astype(F32)
+    first_scale = rms_scale(flat_x)
+    first_normed = (flat_x * first_scale * gain_first).astype(BF)
+    projected = jnp.dot(first_normed, qkv_full, preferred_element_type=F32).astype(BF)
+    mixed, q_aug = attn_fwd(projected, (exq, exk, far_left, far_right), strip, far)
+    middle = flat_x + jnp.dot(mixed, out_full, preferred_element_type=F32)
+    second_scale = rms_scale(middle)
+    second_normed = (middle * second_scale * gain_second).astype(BF)
+    hidden_pre = jnp.dot(second_normed, in_full, preferred_element_type=F32)
+    hidden_float, gate_pullback = jax.vjp(smooth_gate, hidden_pre)
+    hidden = hidden_float.astype(BF)
+    result = middle + jnp.dot(hidden, back_full, preferred_element_type=F32)
+    output = lax.all_to_all(result.astype(BF).reshape(1, seq_len, width), "seq", 1, 0, tiled=True)
+    grad_back = jnp.einsum("tf,td->fd", hidden, g_low, preferred_element_type=F32)
+    grad_hidden = jnp.einsum("td,fd->tf", g_low, back_full, preferred_element_type=F32)
+    grad_pre = gate_pullback(grad_hidden)[0].astype(BF)
+    grad_in = jnp.einsum("td,tf->df", second_normed, grad_pre, preferred_element_type=F32)
+    grad_second_normed = jnp.einsum("tf,df->td", grad_pre, in_full, preferred_element_type=F32)
+    grad_middle_norm, grad_gain_second = norm_backward(
+        middle, second_scale, gain_second, grad_second_normed
+    )
+    grad_middle = g_low.astype(F32) + grad_middle_norm
+    grad_attn = grad_middle.astype(BF)
+    grad_out = jnp.einsum("td,te->de", mixed, grad_attn, preferred_element_type=F32)
+    grad_mixed = jnp.einsum("te,de->td", grad_attn, out_full, preferred_element_type=F32).astype(BF)
+    dq, dk, dv, near, far_sums = attn_bwd(q_aug, projected, grad_mixed, mixed, exk, strip_t)
+    grad_projected = jnp.concatenate([dq, dk, dv], axis=1)
+    grad_qkv = jnp.einsum("td,te->de", first_normed, grad_projected, preferred_element_type=F32)
+    grad_first_normed = jnp.einsum("te,de->td", grad_projected, qkv_full, preferred_element_type=F32)
+    grad_x_norm, grad_gain_first = norm_backward(flat_x, first_scale, gain_first, grad_first_normed)
+    grad_tokens = lax.all_to_all(
+        (grad_middle + grad_x_norm).astype(BF).reshape(1, seq_len, width), "seq", 1, 0, tiled=True
+    )
+    near_bucket = bucket_of(jnp.arange(128)[:, None] + 128 - jnp.arange(384)[None, :])
+    near_hot = (near_bucket[None] == jnp.arange(BUCKETS)[:, None, None]).astype(F32)
+    grad_table = jnp.einsum("bac,hac->bh", near_hot, near, precision=lax.Precision.HIGHEST)
+    query_block = jnp.arange(seq_len)[None, :] // 128
+    key_block = jnp.arange(8)[:, None]
+    left_sum = jnp.sum(jnp.where(key_block <= query_block - 2, far_sums, 0.0), axis=(1, 2))
+    right_sum = jnp.sum(jnp.where(key_block >= query_block + 2, far_sums, 0.0), axis=(1, 2))
+    grad_table = grad_table.at[BUCKETS // 2 - 1].add(left_sum).at[BUCKETS - 1].add(right_sum)
+    axes = ("dp", "seq")
+    small_grad = jnp.concatenate(
+        [
+            grad_gain_first.reshape(n_dev, g_rows),
+            grad_gain_second.reshape(n_dev, g_rows),
+            grad_table.reshape(n_dev, t_rows),
+        ],
+        axis=1,
+    )
+    small_own = lax.psum_scatter(small_grad, axes, scatter_dimension=0, tiled=True)[0]
+    owned = [
+        lax.psum_scatter(g.astype(BF), axes, scatter_dimension=0, tiled=True).astype(F32)
+        for g in (grad_qkv, grad_out, grad_in, grad_back)
+    ]
+    return (
+        output,
+        grad_tokens,
+        small_own[:g_rows],
+        small_own[g_rows : 2 * g_rows],
+        small_own[2 * g_rows :],
+        *owned,
+    )
+
+
 def solution(mesh):
     in_specs = (
         P("dp", "seq", None),
@@ -291,4 +768,4 @@
         P(("dp", "seq"), None),
         P(("dp", "seq"), None),
     )
-    return jax.shard_map(shards, mesh=mesh, in_specs=in_specs, out_specs=out_specs, check_vma=False)
+    return jax.shard_map(fast_shards if fits(mesh) else general_shards, mesh=mesh, in_specs=in_specs, out_specs=out_specs, check_vma=False)

time: 1530 us -> 644 us (0.42)
  waiting for transfers between devices: 847 us -> 216 us
  matrix products: 336 us -> 102 us
  Pallas kernels: 0 us -> 136 us
  other arithmetic: 133 us -> 38.9 us
  local copies, waits for them, and re-layouts: 95 us -> 54 us
  blocking collectives: 96.6 us -> 60.5 us
    reduce_scatter x6 -> x4, waiting for transfers between devices: 594 us -> 212 us  [fast_shards(): lax.psum_scatter(g.astype(BF), axes, scatter_dimension=0, tiled=True)]
    all_gather x6 -> x0, waiting for transfers between devices: 249 us -> none  [the longest x1 107 us: shards(): lax.all_gather(local_values, 'seq', axis=1, tiled=True)]
    dot_general x28 -> x15, matrix products: 336 us -> 102 us  [the longest x1 15.5 us: fast_shards(): jnp.einsum('td,fd->tf', g_low, back_full, preferred_element_type=F32)]
    pallas_call x0 -> x3, Pallas kernels: none -> 136 us  [the longest x1 73.6 us: gather(): pl.pallas_call(functools.partial(gather_kernel, items), out_shape=out_sha...]
    reduce_sum x4 -> x1, other arithmetic: 92.3 us -> 0.19 us  [fast_shards(): jnp.sum(jnp.where(key_block >= query_block + 2, far_sums, 0.0), axis=(1, 2))]
    add x4 -> x5, other arithmetic: 28.5 us -> 1.06 us  [the longest x1 0.89 us: fast_shards(): grad_middle = g_low.astype(F32) + grad_middle_norm]
    while x50 -> x0, local copies, waits for them, and re-layouts: 26.2 us -> none  [the longest x2 19.5 us: shards(): lax.map(attend, (queries, key_groups, value_groups, segquery_groups, segk...]
    unnamed x2 -> x1, blocking collectives: 83.3 us -> 60.5 us
  transfers between devices with their start and end apart: 12 -> 7, of which waited for: 11 -> 3; matrix products, arithmetic and copies ran while one was open for 17% -> 23% of each run, Pallas kernels for 0% -> 10%
where the time goes in v1:
time: 644 us; the launch traced here: 637 us
  waiting for transfers between devices  216 us (34%)
  Pallas kernels  136 us (21%)
  matrix products  102 us (16%)
  blocking collectives  60.5 us (9%)
  local copies, waits for them, and re-layouts  54 us (8%)
  other arithmetic  38.9 us (6%)
  starting transfers between devices  14.6 us (2%)
  between operations  14.5 us (2%)
    reduce_scatter x4, waiting for transfers between devices, fast_shards(): lax.psum_scatter(g.astype(BF), axes, scatter_dimension=0, tiled=True)  212 us
    pallas_call x1, Pallas kernels, gather(): pl.pallas_call(functools.partial(gather_kernel, items), out_shape=out_sha...  73.6 us
    unnamed x1, blocking collectives  60.5 us
    pallas_call x1, Pallas kernels, attn_bwd(): pl.pallas_call(functools.partial(bwd_kernel, nblk), grid=(npair,), in_spe...  36.1 us
    pallas_call x1, Pallas kernels, attn_fwd(): pl.pallas_call(functools.partial(fwd_kernel, nblk), grid=(npair,), in_spe...  26.9 us
    unnamed x66, local copies, waits for them, and re-layouts  25.2 us
    unnamed x4, other arithmetic  22.8 us
    dot_general x1, matrix products, fast_shards(): jnp.einsum('td,fd->tf', g_low, back_full, preferred_element_type=F32)  15.5 us
  transfers between devices with their start and end apart: 7, of which 3 were waited for; matrix products, arithmetic and copies ran while one was open for 23% of the time, Pallas kernels for 10%

profile of v1, /device:TPU:0, one launch (start us, length us, event | category | flops | bytes accessed | tf_op | source)
XLA Modules:
  0.0 636.7 jit_solution(4399672324153419274)
XLA Ops:
  10.5 2.8 broadcast_multiply_fusion
  13.3 73.6 %shard_map.178 = (bf16[4,256,768]{2,1,0:T(8,128)(2,1)}, s32[4,1,256]{2,1,0:T(1,128)}, bf16[32,24,2304]{2,1,0:T(8,128)(2,1)}, bf16[32,24,768]{2,1,0:T(8,128)(2,1)...) custom-call(bf16[4,256,768]{2,1,0:T(8,128)(2,1)} %refs_0_.1, ...), custom_call_target="tpu_custom_call" | custom-call | tf_op jit(solution)/shard_map/pallas_call | solution.py:447
  86.8 4.8 all-to-all-start.1
  96.9 5.6 convolution_convert_fusion.q_ref.k_ref.v_ref
  103.4 26.9 %shard_map.179 = (bf16[1024,768]{1,0:T(8,128)(2,1)S(1)}, bf16[12,1024,128]{2,1,0:T(8,128)(2,1)}) custom-call(f32[12,2]{1,0:T(8,128)S(1)} %copy.108.bl_ref, bf16[1024,2304]{1,0:T(8,128)(2,1)} %convolution_convert_fusion.q_ref.k_ref.v_ref, bf16[1024,2304]{1,0:T(8,128)(2,1)} %convolution_convert_fusion.q_ref.k_ref.v_ref, ...), custom_call_target="tpu_custom_call" | custom-call | flops 12884901888 | bytes 9437184 | tf_op jit(solution)/shard_map/pallas_call | solution.py:542
  130.3 2.9 fusion.8
  135.4 4.2 copy.115.strip_ref
  142.9 8.8 %fusion.50 = f32[1024,3072]{1,0:T(8,128)} fusion(bf16[768,3072]{1,0:T(8,128)(2,1)S(1)} %bitcast.73, f32[1024,768]{0,1:T(8,128)S(1)} %get-tuple-element.102, f32[768]{0:T(1024)S(1)} %reshape.464, f32[1024]{0:T(1024)S(1)} %get-tuple-element.96), kind=kOutput, calls=%fused_computation.130 | convolution fusion | flops 4834197504 | bytes 20454400 | tf_op jit(solution)/shard_map/dot_general | solution.py:689
  153.5 15.5 %fusion.6 = bf16[1024,3072]{1,0:T(8,128)(2,1)S(1)} fusion(f32[1024,3072]{1,0:T(8,128)} %fusion.50, bf16[1024,768]{1,0:T(8,128)(2,1)} %bitcast.12, bf16[3072,768]{1,0:T(8,128)(2,1)} %bitcast.91), kind=kOutput, calls=%fused_computation.8 | convolution fusion | flops 4894752768 | bytes 25165824 | tf_op jit(solution)/shard_map/td,fd->tf/dot_general | solution.py:695
  169.0 10.1 %multiply_reduce_fusion = (f32[768]{0:T(1024)}, f32[1024]{0:T(1024)S(1)}, f32[1024,768]{0,1:T(8,128)S(1)}) fusion(f32[1024,768]{0,1:T(8,128)S(1)} %copy-done.2, f32[1024]{0:T(1024)S(1)} %get-tuple-element.96, f32[768]{0:T(1024)S(1)} %reshape.464, bf16[1024,3072]{1,0:T(8,128)(2,1)S(1)} %fusion.6, bf16[768,3072]{1,0:T(8,128)(2,1)} %bitcast.70), kind=kOutput, calls=%fused_computation.21 | convolution fusion | flops 4836554752 | bytes 17315840 | tf_op jit(solution)/shard_map/tf,df->td/dot_general | solution.py:698
  180.4 2.6 convolution_convert_fusion.4.do_ref
  185.6 36.1 %shard_map.180 = (bf16[1024,768]{1,0:T(8,128)(2,1)S(1)}, bf16[1024,768]{1,0:T(8,128)(2,1)S(1)}, bf16[1024,768]{1,0:T(8,128)(2,1)S(1)}, f32[12,128,384]{2,1,0:T(8,128)}, f32[12,8,1024]{2,1,0:T(8,128)S(1)}) custom-call(bf16[12,1024,128]{2,1,0:T(8,128)(2,1)} %get-tuple-element.59.qa_ref, bf16[1024,2304]{1,0:T(8,128)(2,1)} %convolution_convert_fusion.q_ref.k_ref.v_ref, ...), custom_call_target="tpu_custom_call" | custom-call | flops 32212254720 | bytes 14155776 | tf_op jit(solution)/shard_map/pallas_call | solution.py:621
  225.4 5.4 convolution_convert_fusion.3
  232.7 10.0 %convolution_convert_fusion.2 = bf16[768,3072]{1,0:T(8,128)(2,1)} fusion(bf16[1024,3072]{1,0:T(8,128)(2,1)} %copy-done.24, f32[1024,768]{0,1:T(8,128)S(1)} %copy-done.3, f32[768]{0:T(1024)S(1)} %reshape.464, f32[1024]{0:T(1024)S(1)} %get-tuple-element.96), kind=kOutput, calls=%fused_computation.17 | convolution fusion | flops 4836556800 | bytes 14162944 | tf_op jit(solution)/shard_map/td,tf->df/dot_general | solution.py:697
  242.8 12.1 %convolution_convert_fusion.1 = bf16[3072,768]{1,0:T(8,128)(2,1)} fusion(bf16[1024,768]{1,0:T(8,128)(2,1)} %bitcast.12, f32[1024,3072]{1,0:T(8,128)} %fusion.50), kind=kOutput, calls=%fused_computation.16 | convolution fusion | flops 4862509056 | bytes 18874368 | tf_op jit(solution)/shard_map/tf,td->fd/dot_general | solution.py:694
  254.9 11.2 %fusion.17 = bf16[1,1024,768]{1,2,0:T(8,128)(2,1)} fusion(f32[1024,768]{0,1:T(8,128)S(1)} %copy-done.3, bf16[3072,768]{1,0:T(8,128)(2,1)} %bitcast.92, f32[1024,3072]{1,0:T(8,128)} %fusion.50), kind=kOutput, calls=%fused_computation.41 | convolution fusion | flops 4861722624 | bytes 22020096 | tf_op jit(solution)/shard_map/dot_general | solution.py:692
  266.1 7.6 %copy.112 = bf16[1,1024,768]{2,0,1:T(2,128)(2,1)S(1)} copy(bf16[1,1024,768]{1,2,0:T(8,128)(2,1)} %fusion.17) | data formatting | bytes 3145728 | tf_op jit(solution)/shard_map/reshape | solution.py:693
  274.3 11.4 %reduce.5 = bf16[1024,768]{1,0:T(8,128)(2,1)} reduce(bf16[1024,1,768]{2,1,0:T(2,128)(2,1)S(1)} %bitcast.66, bf16[]{:T(256)} %broadcast.723), dimensions={1}, to_apply=%bitcast.43.reduce_sub_computation | reduce | bytes 3145730
  285.7 3.9 reshape.467
  289.5 5.1 all-to-all-start
  294.6 8.1 %multiply_reduce_fusion.1 = (f32[768]{0:T(1024)}, f32[1024]{0:T(1024)S(1)}, f32[1024,768]{0,1:T(8,128)S(1)}) fusion(f32[1024,768]{0,1:T(8,128)S(1)} %copy-done.6, f32[1024]{0:T(1024)S(1)} %bitcast.85, f32[768]{0:T(1024)S(1)} %reshape.463, bf16[1024,2304]{1,0:T(8,128)(2,1)} %copy-done.15, bf16[768,2304]{1,0:T(8,128)(2,1)} %bitcast.93), kind=kOutput, calls=%fused_computation.22 | convolution fusion | flops 3628595456 | bytes 14563328 | tf_op jit(solution)/shard_map/te,de->td/dot_general | solution.py:709
  304.6 7.4 %copy.119 = bf16[1,1024,768]{2,0,1:T(2,128)(2,1)S(1)} copy(bf16[1,1024,768]{1,2,0:T(8,128)(2,1)} %fusion.14) | data formatting | bytes 3145728 | tf_op jit(solution)/shard_map/reshape | solution.py:712
  312.0 11.4 %reduce.6 = bf16[1024,768]{1,0:T(8,128)(2,1)} reduce(bf16[1024,1,768]{2,1,0:T(2,128)(2,1)S(1)} %bitcast.67, bf16[]{:T(256)} %broadcast.723), dimensions={1}, to_apply=%bitcast.45.reduce_sub_computation | reduce | bytes 3145730
  323.4 3.9 reshape.469
  327.3 4.6 all-to-all-done
  331.9 4.6 all-to-all-start.2
  336.9 4.0 fusion.18
  341.5 3.1 reshape.468
  346.0 60.5 %all-reduce.1 = f32[32,60]{1,0:T(8,128)S(1)} all-reduce(f32[32,60]{1,0:T(8,128)S(1)} %pad_maximum_fusion), channel_id=2, replica_groups=mesh['dp'=8,'seq'=4] {'dp','seq'}, use_global_device_ids=true, to_apply=%region_8.9.clone | all-reduce | flops 1920 | bytes 15360
  409.1 3.1 reshape.470
  415.1 100.8 %reduce-scatter.9.cloned.1.call-done = bf16[24,3072]{1,0:T(8,128)(2,1)} async-done(((bf16[768,3072]{1,0:T(8,128)(2,1)}), bf16[24,3072]{1,0:T(8,128)(2,1)}) %reduce-scatter.9.cloned.1.call-update) | async-done | bytes 147472 | tf_op jit(solution)/shard_map/reduce_scatter | solution.py:733
  517.6 110.7 %reduce-scatter.11.cloned.1.call-done = bf16[96,768]{1,0:T(8,128)(2,1)} async-done(((bf16[3072,768]{1,0:T(8,128)(2,1)}), bf16[96,768]{1,0:T(8,128)(2,1)}) %reduce-scatter.11.cloned.1.call-update) | async-done | bytes 147472 | tf_op jit(solution)/shard_map/reduce_scatter | solution.py:733
  (134 shorter events, 39.8 us)
Async XLA Ops:
  86.8 6.1 copy-start.7
  86.8 64.9 %all-to-all-start.1 = ((bf16[4,256,768]{2,1,0:T(8,128)(2,1)}), bf16[4,256,768]{2,1,0:T(8,128)(2,1)}, u32[]{:S(2)}, u32[]{:S(2)}) async-start(bf16[4,256,768]{2,1,0:T(8,128)(2,1)} %broadcast_multiply_fusion), calls=%async_computation.1 | async-start | bytes 3145728 | tf_op jit(solution)/shard_map/all_to_all | solution.py:676
  91.7 316.0 %reduce-scatter.7.cloned.1.call-start = ((), (), s32[]{:S(2)}) async-start(), calls=%async_computation.8 | async-start | bytes 1216512 | tf_op jit(solution)/shard_map/reduce_scatter | solution.py:733
  92.8 10.3 %copy-start.16 = (s32[1024]{0:T(1024)}, s32[1024]{0:T(1024)S(1)}, u32[]{:S(2)}) copy-start(s32[1024]{0:T(1024)S(1)} %get-tuple-element.110) | copy-start | bytes 12292
  92.8 10.3 %copy-start.18 = (s32[1024]{0:T(1024)}, s32[1024]{0:T(1024)S(1)}, u32[]{:S(2)}) copy-start(s32[1024]{0:T(1024)S(1)} %get-tuple-element.109) | copy-start | bytes 12292
  94.9 2.0 copy-start.23
  95.9 34.4 %copy-start.11 = (s32[128,384]{1,0:T(8,128)}, s32[128,384]{1,0:T(8,128)S(1)}, u32[]{:S(2)}) copy-start(s32[128,384]{1,0:T(8,128)S(1)} %fusion.26) | copy-start | bytes 589828
  96.9 5.6 copy-start.20
  130.3 52.7 %copy-start = (bf16[1024,768]{1,0:T(8,128)(2,1)}, bf16[1024,768]{1,0:T(8,128)(2,1)S(1)}, u32[]{:S(2)}) copy-start(bf16[1024,768]{1,0:T(8,128)(2,1)S(1)} %get-tuple-element.54.o_ref) | copy-start | bytes 4718596
  135.3 4.4 copy-start.13
  135.4 4.3 copy-start.4
  135.4 7.5 %slice-start = ((s8[4718592]{0:T(1024)(128)(4,1)}), s8[4194304]{0:T(1024)(128)(4,1)S(1)}, s32[]{:S(2)}) async-start(s8[4718592]{0:T(1024)(128)(4,1)} %bitcast.71), calls=%async_computation.11 | async-start | bytes 8388608
  139.7 3.2 slice-start.1
  153.5 15.5 %copy-start.2 = (f32[1024,768]{0,1:T(8,128)S(1)}, f32[1024,768]{0,1:T(8,128)}, u32[]{:S(2)}) copy-start(f32[1024,768]{0,1:T(8,128)} %copy-done.1) | copy-start | bytes 9437188
  169.0 10.1 %copy-start.24 = (bf16[1024,3072]{1,0:T(8,128)(2,1)}, bf16[1024,3072]{1,0:T(8,128)(2,1)S(1)}, u32[]{:S(2)}) copy-start(bf16[1024,3072]{1,0:T(8,128)(2,1)S(1)} %fusion.6) | copy-start | bytes 18874372
  180.4 2.6 copy-start.8
  185.5 228.0 %reduce-scatter.5.cloned.1.call-start = ((), (), s32[]{:S(2)}) async-start(), calls=%async_computation.7 | async-start | bytes 3649536 | tf_op jit(solution)/shard_map/reduce_scatter | solution.py:733
  221.8 3.6 copy-start.5
  222.0 2.4 copy-start.15
  230.8 1.9 copy-start.3
  230.8 285.1 %reduce-scatter.9.cloned.1.call-start = ((), (), s32[]{:S(2)}) async-start(), calls=%async_computation.9 | async-start | bytes 4866048 | tf_op jit(solution)/shard_map/reduce_scatter | solution.py:733
  242.7 385.6 %reduce-scatter.11.cloned.1.call-start = ((), (), s32[]{:S(2)}) async-start(), calls=%async_computation.10 | async-start | bytes 4866048 | tf_op jit(solution)/shard_map/reduce_scatter | solution.py:733
  285.7 8.9 %copy-start.6 = (f32[1024,768]{0,1:T(8,128)S(1)}, f32[1024,768]{0,1:T(8,128)}, u32[]{:S(2)}) copy-start(f32[1024,768]{0,1:T(8,128)} %copy.110) | copy-start | bytes 9437188
  289.5 42.4 %all-to-all-start = ((bf16[4,2,98304]{2,1,0:T(2,128)(2,1)}), bf16[4,2,98304]{2,1,0:T(2,128)(2,1)}, u32[]{:S(2)}, u32[]{:S(2)}) async-start(bf16[4,2,98304]{2,1,0:T(2,128)(2,1)} %reshape.467), calls=%async_computation | async-start | bytes 3145728 | tf_op jit(solution)/shard_map/all_to_all | solution.py:693
  294.6 8.1 %copy-start.9 = (f32[1024,768]{0,1:T(8,128)S(1)}, f32[1024,768]{0,1:T(8,128)}, u32[]{:S(2)}) copy-start(f32[1024,768]{0,1:T(8,128)} %copy-done.8) | copy-start | bytes 9437188
  323.4 13.0 %copy-start.19 = (s32[1024]{0:T(1024)S(1)}, s32[1024]{0:T(1024)}, u32[]{:S(2)}) copy-start(s32[1024]{0:T(1024)} %copy-done.18) | copy-start | bytes 12292
  323.4 13.1 %copy-start.17 = (s32[1024]{0:T(1024)S(1)}, s32[1024]{0:T(1024)}, u32[]{:S(2)}) copy-start(s32[1024]{0:T(1024)} %copy-done.16) | copy-start | bytes 12292
  323.4 13.5 %copy-start.10 = (f32[12,128,384]{2,1,0:T(8,128)S(1)}, f32[12,128,384]{2,1,0:T(8,128)}, u32[]{:S(2)}) copy-start(f32[12,128,384]{2,1,0:T(8,128)} %get-tuple-element.63) | copy-start | bytes 7077892
  323.4 13.5 %copy-start.12 = (s32[128,384]{1,0:T(8,128)S(1)}, s32[128,384]{1,0:T(8,128)}, u32[]{:S(2)}) copy-start(s32[128,384]{1,0:T(8,128)} %copy-done.11) | copy-start | bytes 589828
  327.3 14.0 %copy-start.22 = (f32[768]{0:T(1024)S(1)}, f32[768]{0:T(1024)}, u32[]{:S(2)}) copy-start(f32[768]{0:T(1024)} %get-tuple-element.83) | copy-start | bytes 9220
  327.3 14.1 %copy-start.21 = (f32[768]{0:T(1024)S(1)}, f32[768]{0:T(1024)}, u32[]{:S(2)}) copy-start(f32[768]{0:T(1024)} %get-tuple-element.85) | copy-start | bytes 9220
  331.9 77.2 %all-to-all-start.2 = ((bf16[4,2,98304]{2,1,0:T(2,128)(2,1)}), bf16[4,2,98304]{2,1,0:T(2,128)(2,1)}, u32[]{:S(2)}, u32[]{:S(2)}) async-start(bf16[4,2,98304]{2,1,0:T(2,128)(2,1)} %reshape.469), calls=%async_computation.2 | async-start | bytes 3145728 | tf_op jit(solution)/shard_map/all_to_all | solution.py:711
  (2 other events, 2.9 us)
Sparse Core Ops, SparseCore 0:
  185.7 96.6 reduce-scatter.6
  287.8 116.5 reduce-scatter.4
  409.9 105.9 reduce-scatter.8
  522.2 106.0 reduce-scatter.10

commit v2 on v1

--- a/solution.py
+++ b/solution.py
@@ -630,11 +630,287 @@
     )(qa, qkv, qkv, do, o, exk, stripT)
 
 
+GELU_A = 0.7978845608028654
+GELU_B = 0.044715
+
+
+def mm(a, b, dims=((1,), (0,))):
+    return lax.dot_general(a, b, (dims, ((), ())), preferred_element_type=F32)
+
+
+def ffn_kernel(x_ref, mixed_ref, g_ref, gain_ref, wo_ref, wi_ref, wb_ref,
+               out_ref, gm_ref, gmix_ref, dwo_ref, dwi_ref, dwb_ref, dgain_ref,
+               mid_ref, h_ref, ht_ref, acc_ref, dh_ref):
+    step = pl.program_id(0)
+    rows = x_ref.shape[0]
+    half = 256
+
+    @pl.when(step == 0)
+    def _():
+        for r in range(0, rows, half):
+            part = pl.ds(r, half)
+            middle = x_ref[part].astype(F32) + mm(mixed_ref[part], wo_ref[...])
+            mid_ref[part] = middle
+            acc_ref[part] = middle
+            scale = lax.rsqrt(jnp.mean(middle * middle, axis=-1, keepdims=True) + EPS)
+            normed = (middle * scale * gain_ref[...]).astype(BF)
+            h_ref[part] = normed
+            ht_ref[:, part] = normed.T
+            dh_ref[part] = jnp.zeros((half, x_ref.shape[1]), F32)
+
+    gates = []
+    hiddens = []
+    for r in range(0, rows, half):
+        part = pl.ds(r, half)
+        pre = mm(h_ref[part], wi_ref[...])
+        dhid = mm(g_ref[part], wb_ref[...], ((1,), (1,)))
+        sq = pre * pre
+        t = jnp.tanh(pre * (GELU_A + GELU_A * GELU_B * sq))
+        half_t = 0.5 + 0.5 * t
+        hidden = (pre * half_t).astype(BF)
+        slope = half_t + pre * (0.5 - 0.5 * t * t) * (GELU_A + 3.0 * GELU_A * GELU_B * sq)
+        dpre = (dhid * slope).astype(BF)
+        acc_ref[part] += mm(hidden, wb_ref[...])
+        dh_ref[part] += mm(dpre, wi_ref[...], ((1,), (1,)))
+        hiddens.append(hidden)
+        gates.append(dpre)
+    dwi_ref[...] = mm(ht_ref[...], jnp.concatenate(gates, axis=0)).astype(BF)
+    dwb_ref[...] = mm(jnp.concatenate(hiddens, axis=0), g_ref[...], ((0,), (0,))).astype(BF)
+
+    @pl.when(step == pl.num_programs(0) - 1)
+    def _():
+        dgain = jnp.zeros((1, x_ref.shape[1]), F32)
+        for r in range(0, rows, half):
+            part = pl.ds(r, half)
+            out_ref[part] = acc_ref[part].astype(BF)
+            middle = mid_ref[part]
+            dh = dh_ref[part]
+            scale = lax.rsqrt(jnp.mean(middle * middle, axis=-1, keepdims=True) + EPS)
+            dgain += jnp.sum(dh * (middle * scale), axis=0, keepdims=True)
+            u = dh * gain_ref[...]
+            inner = jnp.mean(u * middle, axis=-1, keepdims=True)
+            gm = g_ref[part].astype(F32) + scale * u - middle * (scale * scale * scale * inner)
+            gm_ref[part] = gm
+            low = gm.astype(BF)
+            h_ref[part] = low
+            gmix_ref[part] = mm(low, wo_ref[...], ((1,), (1,))).astype(BF)
+        dgain_ref[...] = dgain
+        dwo_ref[...] = mm(mixed_ref[...], h_ref[...], ((0,), (0,))).astype(BF)
+
+
+def ffn(x, mixed, g, gain, wo, wi, wb, chunk=512):
+    rows, width = x.shape
+    ff = wi.shape[1]
+    whole = lambda s: pl.BlockSpec(s, lambda i: (0, 0), pipeline_mode=pl.Buffered(1))
+    S = jax.ShapeDtypeStruct
+    return pl.pallas_call(
+        ffn_kernel,
+        grid=(ff // chunk,),
+        in_specs=[whole((rows, width))] * 3 + [whole((1, width)), whole((width, width)),
+                  pl.BlockSpec((width, chunk), lambda i: (0, i)), pl.BlockSpec((chunk, width), lambda i: (i, 0))],
+        out_specs=[whole((rows, width))] * 3 + [whole((width, width)), pl.BlockSpec((width, chunk), lambda i: (0, i)),
+                   pl.BlockSpec((chunk, width), lambda i: (i, 0)), whole((1, width))],
+        out_shape=[S((rows, width), BF), S((rows, width), F32), S((rows, width), BF), S((width, width), BF),
+                   S((width, ff), BF), S((ff, width), BF), S((1, width), F32)],
+        scratch_shapes=[pltpu.VMEM((rows, width), F32), pltpu.VMEM((rows, width), BF), pltpu.VMEM((width, rows), BF),
+                        pltpu.VMEM((rows, width), F32), pltpu.VMEM((rows, width), F32)],
+        compiler_params=pltpu.CompilerParams(vmem_limit_bytes=56 << 20),
+        cost_estimate=pl.CostEstimate(flops=12 * rows * width * ff + 6 * rows * width * width, bytes_accessed=50 << 20, transcendentals=rows * ff),
+    )(x, mixed, g, gain, wo, wi, wb)
+
+
+def tail_kernel(dq_ref, dk_ref, dv_ref, x_ref, gm_ref, gain_ref, w_ref, gx_ref, dw_ref, dgain_ref, ht_ref):
+    rows, width = x_ref.shape
+    half = 256
+    dgain = jnp.zeros((1, width), F32)
+    for r in range(0, rows, half):
+        part = pl.ds(r, half)
+        x = x_ref[part].astype(F32)
+        scale = lax.rsqrt(jnp.mean(x * x, axis=-1, keepdims=True) + EPS)
+        ht_ref[:, part] = (x * scale * gain_ref[...]).astype(BF).T
+        dh = sum(mm(d[part], w_ref[:, i * width:(i + 1) * width], ((1,), (1,))) for i, d in enumerate((dq_ref, dk_ref, dv_ref)))
+        dgain += jnp.sum(dh * (x * scale), axis=0, keepdims=True)
+        u = dh * gain_ref[...]
+        inner = jnp.mean(u * x, axis=-1, keepdims=True)
+        gx_ref[part] = (gm_ref[part] + scale * u - x * (scale * scale * scale * inner)).astype(BF)
+    dgain_ref[...] = dgain
+    for i, d in enumerate((dq_ref, dk_ref, dv_ref)):
+        dw_ref[:, i * width:(i + 1) * width] = mm(ht_ref[...], d[...]).astype(BF)
+
+
+def tail(dq, dk, dv, x, gm, gain, w):
+    rows, width = x.shape
+    S = jax.ShapeDtypeStruct
+    return pl.pallas_call(
+        tail_kernel,
+        out_shape=[S((rows, width), BF), S((width, 3 * width), BF), S((1, width), F32)],
+        scratch_shapes=[pltpu.VMEM((width, rows), BF)],
+        compiler_params=pltpu.CompilerParams(vmem_limit_bytes=56 << 20),
+        cost_estimate=pl.CostEstimate(flops=12 * rows * width * width, bytes_accessed=24 << 20, transcendentals=0),
+    )(dq, dk, dv, x, gm, gain, w)
+
+
+def scatter_kernel(routes, *refs):
+    n_it = len(routes)
+    n_z = 4
+    gx = refs[0]
+    part = refs[1:1 + n_it]
+    gx_out = refs[1 + n_it]
+    outs = refs[2 + n_it:2 + 2 * n_it]
+    scr = refs[2 + 2 * n_it:]
+    rc, r2, r1, zo, zu, zd = (scr[k * n_it:(k + 1) * n_it] for k in range(6))
+    loc_sem, t_send, t_recv, c_send, c_recv, x2_send, x2_recv, x1_send, x1_recv, z_send, z_recv = scr[6 * n_it:]
+    dp, z = lax.axis_index("dp"), lax.axis_index("seq")
+    core = lax.rem(dp, 2)
+    quad = dp // 2
+    peers = [(dp, lax.rem(z + s, n_z)) for s in range(1, n_z)] + [(flip(dp, b), z) for b in (1, 2, 4)]
+    barrier = pltpu.get_barrier_semaphore()
+    for p in peers:
+        pl.semaphore_signal(barrier, inc=1, device_id=p, device_id_type=MESH)
+    pl.semaphore_wait(barrier, len(peers))
+
+    def remote(src, dst, ss, rs, to):
+        return pltpu.make_async_remote_copy(src_ref=src, dst_ref=dst, send_sem=ss, recv_sem=rs, device_id=to, device_id_type=MESH)
+
+    def add_into(dst, src, chunk=16):
+        rows = dst.shape[0]
+        chunk = min(chunk, rows)
+        @pl.loop(0, rows // chunk)
+        def _(i):
+            at = pl.ds(pl.multiple_of(i * chunk, chunk), chunk)
+            dst[at] = (dst[at].astype(F32) + src[at].astype(F32)).astype(dst.dtype)
+
+    def q_at(it, f1, f2):
+        b1, b2 = routes[it]
+        q = quad
+        if f1: q = flip(q, b1 // 2)
+        if f2: q = flip(q, b2 // 2)
+        return q
+
+    def c_copy(it, q):
+        return remote(part[it].at[2 * q + 1 - core], rc[it].at[q], c_send.at[it, q], c_recv.at[it, q], (flip(dp, 1), z))
+
+    def x2_copy(it, f1):
+        q = q_at(it, f1, True)
+        k = (q // (routes[it][0] // 2)) % 2
+        return remote(rc[it].at[q], r2[it].at[k], x2_send.at[it, k], x2_recv.at[it, k], (flip(dp, routes[it][1]), z))
+
+    def x2_slot(it, f1):
+        return (q_at(it, f1, False) // (routes[it][0] // 2)) % 2
+
+    def x1_copy(it):
+        return remote(rc[it].at[q_at(it, True, False)], r1[it], x1_send.at[it], x1_recv.at[it], (flip(dp, routes[it][0]), z))
+
+    def tok_copy(s):
+        to = lax.rem(z + s, n_z)
+        return remote(gx.at[to], gx_out.at[z], t_send.at[s - 1], t_recv.at[s - 1], (dp, to))
+
+    for it in range(n_it):
+        for f1, f2 in ((False, True), (True, True), (True, False), (False, False)):
+            c_copy(it, q_at(it, f1, f2)).start()
+    loc = pltpu.make_async_copy(gx.at[z], gx_out.at[z], loc_sem.at[0])
+    loc.start()
+    for s in range(1, n_z):
+        tok_copy(s).start()
+
+    def core_sum(it, f1, f2):
+        q = q_at(it, f1, f2)
+        c_copy(it, q).wait_recv()
+        add_into(rc[it].at[q], part[it].at[2 * q + core])
+
+    for it in range(n_it):
+        for f1 in (True, False):
+            core_sum(it, f1, True)
+            x2_copy(it, f1).start()
+    for it in range(n_it):
+        core_sum(it, True, False)
+        core_sum(it, False, False)
+    for it in range(n_it):
+        for f1 in (True, False):
+            k = x2_slot(it, f1)
+            remote(rc[it].at[0], r2[it].at[k], x2_send.at[it, k], x2_recv.at[it, k], (dp, z)).wait_recv()
+            add_into(rc[it].at[q_at(it, f1, False)], r2[it].at[k])
+            if f1:
+                x1_copy(it).start()
+
+    def z_copy(it, way, j):
+        src = zo[it].at[j]
+        dst = (zu if way == 0 else zd)[it].at[j]
+        return remote(src, dst, z_send.at[it, way, j], z_recv.at[it, way, j], (dp, z + 1 if way == 0 else z - 1))
+
+    def z_wait(it, way, j):
+        buf = (zu if way == 0 else zd)[it].at[j]
+        remote(buf, buf, z_send.at[it, way, j], z_recv.at[it, way, j], (dp, z)).wait_recv()
+
+    for it in range(n_it):
+        x1_copy(it).wait_recv()
+        rows = zo[it].shape[1]
+        for j in range(n_z):
+            at = pl.ds(j * rows, rows)
+            zo[it][j] = (rc[it][quad, at].astype(F32) + r1[it][at].astype(F32)).astype(zo[it].dtype)
+        for k in range(n_z - 1):
+            for way, j in ((0, n_z - 1 - k), (1, k)):
+                ahead, behind = (j > z, z > 0) if way == 0 else (j < z, z < n_z - 1)
+                @pl.when(ahead)
+                def _():
+                    @pl.when(behind)
+                    def _():
+                        z_wait(it, way, j)
+                        buf = (zu if way == 0 else zd)[it]
+                        zo[it][j] = (zo[it][j].astype(F32) + buf[j].astype(F32)).astype(zo[it].dtype)
+                    z_copy(it, way, j).start()
+    for it in range(n_it):
+        outs[it][...] = zo[it][z].astype(F32)
+        @pl.when(z > 0)
+        def _():
+            z_wait(it, 0, z)
+            outs[it][...] += zu[it][z].astype(F32)
+        @pl.when(z < n_z - 1)
+        def _():
+            z_wait(it, 1, z)
+            outs[it][...] += zd[it][z].astype(F32)
+    for s in range(1, n_z):
+        frm = lax.rem(z + n_z - s, n_z)
+        remote(gx_out.at[frm], gx_out.at[frm], t_send.at[s - 1], t_recv.at[s - 1], (dp, z)).wait_recv()
+    loc.wait()
+    for s in range(1, n_z):
+        tok_copy(s).wait_send()
+    for it in range(n_it):
+        for q in range(4):
+            c_copy(it, q).wait_send()
+        for f1 in (True, False):
+            x2_copy(it, f1).wait_send()
+        x1_copy(it).wait_send()
+        for j in range(n_z):
+            for way in (0, 1):
+                @pl.when(j > z if way == 0 else j < z)
+                def _():
+                    z_copy(it, way, j).wait_send()
+
+def scatter(gx, parts, routes, collective_id=1):
+    n_it = len(parts)
+    D = pltpu.SemaphoreType.DMA
+    V = lambda p, *lead: pltpu.VMEM((*lead, *p.shape[1:]), p.dtype)
+    zs = lambda p: pltpu.VMEM((4, p.shape[1] // 4, p.shape[2]), p.dtype)
+    vm = pl.BlockSpec(memory_space=pltpu.VMEM)
+    scratch = [V(p, 4) for p in parts] + [V(p, 2) for p in parts] + [V(p) for p in parts] + [zs(p) for p in parts] * 3
+    scratch += [D((1,)), D((3,)), D((3,)), D((n_it, 4)), D((n_it, 4)), D((n_it, 2)), D((n_it, 2)), D((n_it,)), D((n_it,)), D((n_it, 2, 4)), D((n_it, 2, 4))]
+    return pl.pallas_call(
+        functools.partial(scatter_kernel, routes),
+        out_shape=[jax.ShapeDtypeStruct(gx.shape, gx.dtype)] + [jax.ShapeDtypeStruct((p.shape[1] // 4, p.shape[2]), F32) for p in parts],
+        in_specs=[vm] * (1 + n_it),
+        out_specs=[pl.BlockSpec(memory_space=pltpu.HBM)] + [vm] * n_it,
+        scratch_shapes=scratch,
+        compiler_params=pltpu.CompilerParams(collective_id=collective_id, has_side_effects=True, vmem_limit_bytes=56 << 20),
+    )(gx, *parts)
+
+
 def fits(mesh):
     return mesh.shape["dp"] == 8 and mesh.shape["seq"] == 4
 
 
 ITEMS = ((0, 4, 2), (4, 2, 4), (1, 2, 4), (2, 4, 2), (3, 2, 4))
+ROUTES = ((4, 2), (2, 4), (2, 4), (4, 2), (2, 4))
 
 
 def fast_shards(
@@ -674,43 +950,21 @@
     table = small_full[:, 2 * g_rows : 2 * g_rows + t_rows].reshape(BUCKETS, HEADS)
     grad_local, x4 = lax.optimization_barrier((grad_local, x4))
     g_low = lax.all_to_all(grad_local, "seq", 0, 1, tiled=True).reshape(seq_len, width)
-    flat_x = x4.reshape(seq_len, width).astype(F32)
+    x = x4.reshape(seq_len, width)
+    flat_x = x.astype(F32)
     seg = seg4.reshape(seq_len)
     exq, exk, far_left, far_right = extras(seg)
     strip, strip_t = strips(table.astype(F32))
     far = jnp.stack([table[BUCKETS // 2 - 1], table[BUCKETS - 1]], axis=1).astype(F32)
-    first_scale = rms_scale(flat_x)
-    first_normed = (flat_x * first_scale * gain_first).astype(BF)
+    first_normed = (flat_x * rms_scale(flat_x) * gain_first).astype(BF)
     projected = jnp.dot(first_normed, qkv_full, preferred_element_type=F32).astype(BF)
     mixed, q_aug = attn_fwd(projected, (exq, exk, far_left, far_right), strip, far)
-    middle = flat_x + jnp.dot(mixed, out_full, preferred_element_type=F32)
-    second_scale = rms_scale(middle)
-    second_normed = (middle * second_scale * gain_second).astype(BF)
-    hidden_pre = jnp.dot(second_normed, in_full, preferred_element_type=F32)
-    hidden_float, gate_pullback = jax.vjp(smooth_gate, hidden_pre)
-    hidden = hidden_float.astype(BF)
-    result = middle + jnp.dot(hidden, back_full, preferred_element_type=F32)
-    output = lax.all_to_all(result.astype(BF).reshape(1, seq_len, width), "seq", 1, 0, tiled=True)
-    grad_back = jnp.einsum("tf,td->fd", hidden, g_low, preferred_element_type=F32)
-    grad_hidden = jnp.einsum("td,fd->tf", g_low, back_full, preferred_element_type=F32)
-    grad_pre = gate_pullback(grad_hidden)[0].astype(BF)
-    grad_in = jnp.einsum("td,tf->df", second_normed, grad_pre, preferred_element_type=F32)
-    grad_second_normed = jnp.einsum("tf,df->td", grad_pre, in_full, preferred_element_type=F32)
-    grad_middle_norm, grad_gain_second = norm_backward(
-        middle, second_scale, gain_second, grad_second_normed
-    )
-    grad_middle = g_low.astype(F32) + grad_middle_norm
-    grad_attn = grad_middle.astype(BF)
-    grad_out = jnp.einsum("td,te->de", mixed, grad_attn, preferred_element_type=F32)
-    grad_mixed = jnp.einsum("te,de->td", grad_attn, out_full, preferred_element_type=F32).astype(BF)
+    result, grad_middle, grad_mixed, grad_out, grad_in, grad_back, grad_gain_second = ffn(
+        x, mixed, g_low, gain_second, out_full, in_full, back_full
+    )
+    output = lax.all_to_all(result.reshape(1, seq_len, width), "seq", 1, 0, tiled=True)
     dq, dk, dv, near, far_sums = attn_bwd(q_aug, projected, grad_mixed, mixed, exk, strip_t)
-    grad_projected = jnp.concatenate([dq, dk, dv], axis=1)
-    grad_qkv = jnp.einsum("td,te->de", first_normed, grad_projected, preferred_element_type=F32)
-    grad_first_normed = jnp.einsum("te,de->td", grad_projected, qkv_full, preferred_element_type=F32)
-    grad_x_norm, grad_gain_first = norm_backward(flat_x, first_scale, gain_first, grad_first_normed)
-    grad_tokens = lax.all_to_all(
-        (grad_middle + grad_x_norm).astype(BF).reshape(1, seq_len, width), "seq", 1, 0, tiled=True
-    )
+    grad_x, grad_qkv, grad_gain_first = tail(dq, dk, dv, x, grad_middle, gain_first, qkv_full)
     near_bucket = bucket_of(jnp.arange(128)[:, None] + 128 - jnp.arange(384)[None, :])
     near_hot = (near_bucket[None] == jnp.arange(BUCKETS)[:, None, None]).astype(F32)
     grad_table = jnp.einsum("bac,hac->bh", near_hot, near, precision=lax.Precision.HIGHEST)
@@ -719,7 +973,6 @@
     left_sum = jnp.sum(jnp.where(key_block <= query_block - 2, far_sums, 0.0), axis=(1, 2))
     right_sum = jnp.sum(jnp.where(key_block >= query_block + 2, far_sums, 0.0), axis=(1, 2))
     grad_table = grad_table.at[BUCKETS // 2 - 1].add(left_sum).at[BUCKETS - 1].add(right_sum)
-    axes = ("dp", "seq")
     small_grad = jnp.concatenate(
         [
             grad_gain_first.reshape(n_dev, g_rows),
@@ -728,18 +981,24 @@
         ],
         axis=1,
     )
-    small_own = lax.psum_scatter(small_grad, axes, scatter_dimension=0, tiled=True)[0]
-    owned = [
-        lax.psum_scatter(g.astype(BF), axes, scatter_dimension=0, tiled=True).astype(F32)
-        for g in (grad_qkv, grad_out, grad_in, grad_back)
-    ]
+    small_grad = jnp.pad(small_grad[:, None], ((0, 0), (0, 7), (0, 128 - small_grad.shape[1])))
+    parts = (grad_qkv, small_grad.reshape(n_dev * 8, 128), grad_out, grad_in, grad_back)
+    grad_tokens, own_qkv, own_small, own_out, own_in, own_back = scatter(
+        grad_x.reshape(n_z, block_len, width),
+        [p.reshape(8, -1, p.shape[1]) for p in parts],
+        ROUTES,
+    )
+    own_small = own_small[0]
     return (
         output,
         grad_tokens,
-        small_own[:g_rows],
-        small_own[g_rows : 2 * g_rows],
-        small_own[2 * g_rows :],
-        *owned,
+        own_small[:g_rows],
+        own_small[g_rows : 2 * g_rows],
+        own_small[2 * g_rows : 2 * g_rows + t_rows],
+        own_qkv,
+        own_out,
+        own_in,
+        own_back,
     )
 
 

time: 644 us -> 394 us (0.61)
  waiting for transfers between devices: 216 us -> 0.01 us
  Pallas kernels: 136 us -> 306 us
  matrix products: 102 us -> 16.9 us
  blocking collectives: 60.5 us -> 0 us
  other arithmetic: 38.9 us -> 19.3 us
  local copies, waits for them, and re-layouts: 54 us -> 36.8 us
  between operations: 14.5 us -> 1.39 us
    reduce_scatter x4 -> x0, waiting for transfers between devices: 212 us -> none  [fast_shards(): lax.psum_scatter(g.astype(BF), axes, scatter_dimension=0, tiled=True)]
    pallas_call x0 -> x3, Pallas kernels: none -> 169 us  [the longest x1 109 us: scatter(): pl.pallas_call(functools.partial(scatter_kernel, routes), out_shape=[jax....]
    dot_general x11 -> x0, matrix products: 88 us -> none  [the longest x1 15.5 us: fast_shards(): jnp.einsum('td,fd->tf', g_low, back_full, preferred_element_type=F32)]
    unnamed x1 -> x0, blocking collectives: 60.5 us -> none
    reshape x3 -> x1, local copies, waits for them, and re-layouts: 16.7 us -> 3.84 us  [fast_shards(): result.reshape(1, seq_len, width)]
    unnamed x4 -> x1, other arithmetic: 22.8 us -> 11.6 us
    unnamed x66 -> x42, local copies, waits for them, and re-layouts: 25.2 us -> 17.7 us
  transfers between devices with their start and end apart: 7 -> 2, of which waited for: 3 -> 0; matrix products, arithmetic and copies ran while one was open for 23% -> 9% of each run, Pallas kernels for 10% -> 48%
where the time goes in v2:
time: 394 us; the launch traced here: 390 us
  Pallas kernels  306 us (78%)
  local copies, waits for them, and re-layouts  36.8 us (9%)
  other arithmetic  19.3 us (5%)
  matrix products  16.9 us (4%)
  starting transfers between devices  10.1 us (3%)
    pallas_call x1, Pallas kernels, scatter(): pl.pallas_call(functools.partial(scatter_kernel, routes), out_shape=[jax....  109 us
    pallas_call x1, Pallas kernels, gather(): pl.pallas_call(functools.partial(gather_kernel, items), out_shape=out_sha...  73.6 us
    pallas_call x1, Pallas kernels, ffn(): pl.pallas_call(ffn_kernel, grid=(ff // chunk,), in_specs=[whole((rows, wi...  45.2 us
    pallas_call x1, Pallas kernels, attn_bwd(): pl.pallas_call(functools.partial(bwd_kernel, nblk), grid=(npair,), in_spe...  36.1 us
    pallas_call x1, Pallas kernels, attn_fwd(): pl.pallas_call(functools.partial(fwd_kernel, nblk), grid=(npair,), in_spe...  27 us
    unnamed x42, local copies, waits for them, and re-layouts  17.7 us
    pallas_call x1, Pallas kernels, tail(): pl.pallas_call(tail_kernel, out_shape=[S((rows, width), BF), S((width, 3...  14.6 us
    unnamed x1, other arithmetic  11.6 us
  transfers between devices with their start and end apart: 2, of which 0 were waited for; matrix products, arithmetic and copies ran while one was open for 9% of the time, Pallas kernels for 48%

profile of v2, /device:TPU:0, one launch (start us, length us, event | category | flops | bytes accessed | tf_op | source)
XLA Modules:
  0.0 390.3 jit_solution(3495628573849116123)
XLA Ops:
  0.6 1.3 reshape.436.refs_1_
  2.6 0.8 maximum_bitcast_fusion
  4.0 2.8 broadcast_multiply_fusion
  6.7 73.6 %shard_map.178 = (bf16[4,256,768]{2,1,0:T(8,128)(2,1)}, s32[4,1,256]{2,1,0:T(1,128)}, bf16[32,24,2304]{2,1,0:T(8,128)(2,1)}, bf16[32,24,768]{2,1,0:T(8,128)(2,1)...) custom-call(bf16[4,256,768]{2,1,0:T(8,128)(2,1)} %refs_0_.1, ...), custom_call_target="tpu_custom_call" | custom-call | tf_op jit(solution)/shard_map/pallas_call | solution.py:447
  80.3 5.1 %all-to-all-start = ((bf16[4,256,768]{2,1,0:T(8,128)(2,1)}), bf16[4,256,768]{2,1,0:T(8,128)(2,1)}, u32[]{:S(2)}, u32[]{:S(2)}) async-start(bf16[4,256,768]{2,1,0:T(8,128)(2,1)} %broadcast_multiply_fusion), calls=%async_computation | async-start | bytes 3145728 | tf_op jit(solution)/shard_map/all_to_all | solution.py:952
  85.4 0.9 slice.76
  87.1 2.9 fusion.2
  90.3 2.9 fusion.1
  95.1 2.6 copy.62.strip_ref
  98.4 4.2 %copy.64.strip_ref = f32[12,128,384]{2,1,0:T(8,128)} copy(f32[12,128,384]{2,0,1:T(8,128)} %fusion.1) | data formatting | bytes 4718592 | tf_op jit(solution)/shard_map/bac,bh->hac/dot_general | solution.py:487
  103.0 5.5 %convolution_convert_fusion.q_ref.k_ref.v_ref = bf16[1024,2304]{1,0:T(8,128)(2,1)} fusion(bf16[1024,768]{1,0:T(8,128)(2,1)S(1)} %bitcast.58, bf16[768,2304]{1,0:T(8,128)(2,1)S(1)} %bitcast.76), kind=kOutput, calls=%fused_computation.5 | convolution fusion | flops 3626237952 | bytes 9830400 | tf_op jit(solution)/shard_map/dot_general | solution.py:960
  108.5 27.0 %shard_map.179 = (bf16[1024,768]{1,0:T(8,128)(2,1)S(1)}, bf16[12,1024,128]{2,1,0:T(8,128)(2,1)}) custom-call(f32[12,2]{1,0:T(8,128)S(1)} %copy.61.bl_ref, bf16[1024,2304]{1,0:T(8,128)(2,1)} %convolution_convert_fusion.q_ref.k_ref.v_ref, bf16[1024,2304]{1,0:T(8,128)(2,1)} %convolution_convert_fusion.q_ref.k_ref.v_ref, ...), custom_call_target="tpu_custom_call" | custom-call | flops 12884901888 | bytes 9437184 | tf_op jit(solution)/shard_map/pallas_call | solution.py:542
  135.5 1.1 copy-done.3
  136.6 45.2 %shard_map.180 = (bf16[1024,768]{1,0:T(8,128)(2,1)}, f32[1024,768]{1,0:T(8,128)}, bf16[1024,768]{1,0:T(8,128)(2,1)}, bf16[768,768]{1,0:T(8,128)(2,1)}, bf16[768,...) custom-call(bf16[1024,768]{1,0:T(8,128)(2,1)} %bitcast.53, bf16[1024,768]{1,0:T(8,128)(2,1)} %copy-done.3, ...), custom_call_target="tpu_custom_call" | custom-call | flops 32614907904 | bytes 52428800 | tf_op jit(solution)/shard_map/pallas_call | solution.py:706
  181.8 3.8 copy.82
  186.1 11.6 %reduce.7 = bf16[1024,768]{1,0:T(8,128)(2,1)} reduce(bf16[1024,1,768]{2,1,0:T(2,128)(2,1)S(1)} %bitcast.51, bf16[]{:T(256)} %broadcast.625), dimensions={1}, to_apply=%bitcast.50.reduce_sub_computation | reduce | bytes 3145730
  197.7 3.7 reshape.460
  201.4 5.1 %all-to-all-start.1 = ((bf16[4,2,98304]{2,1,0:T(2,128)(2,1)}), bf16[4,2,98304]{2,1,0:T(2,128)(2,1)}, u32[]{:S(2)}, u32[]{:S(2)}) async-start(bf16[4,2,98304]{2,1,0:T(2,128)(2,1)} %reshape.460), calls=%async_computation.1 | async-start | bytes 3145728 | tf_op jit(solution)/shard_map/all_to_all | solution.py:965
  206.5 36.1 %shard_map.181 = (bf16[1024,768]{1,0:T(8,128)(2,1)S(1)}, bf16[1024,768]{1,0:T(8,128)(2,1)S(1)}, bf16[1024,768]{1,0:T(8,128)(2,1)S(1)}, f32[12,128,384]{2,1,0:T(8,128)}, f32[12,8,1024]{2,1,0:T(8,128)S(1)}) custom-call(bf16[12,1024,128]{2,1,0:T(8,128)(2,1)} %get-tuple-element.76.qa_ref, bf16[1024,2304]{1,0:T(8,128)(2,1)} %convolution_convert_fusion.q_ref.k_ref.v_ref, ...), custom_call_target="tpu_custom_call" | custom-call | flops 32212254720 | bytes 14155776 | tf_op jit(solution)/shard_map/pallas_call | solution.py:621
  242.6 1.1 copy-done
  243.8 1.1 copy-done.1
  244.9 1.1 copy-done.2
  246.4 5.6 %fusion.10 = f32[32,12]{0,1:T(8,128)S(1)} fusion(f32[12,128,384]{2,1,0:T(8,128)} %get-tuple-element.86, s32[128,384]{1,0:T(8,128)S(1)} %copy-done.7), kind=kOutput, calls=%fused_computation.15 | convolution fusion | flops 228065280 | bytes 2557440 | tf_op jit(solution)/shard_map/bac,hac->bh/dot_general | solution.py:970
  252.7 14.6 %shard_map.182 = (bf16[1024,768]{1,0:T(8,128)(2,1)}, bf16[768,2304]{1,0:T(8,128)(2,1)}, f32[1,768]{1,0:T(1,128)}) custom-call(bf16[1024,768]{1,0:T(8,128)(2,1)} %copy-done, bf16[1024,768]{1,0:T(8,128)(2,1)} %copy-done.1, bf16[1024,768]{1,0:T(8,128)(2,1)} %copy-done.2, bf16[1024,768]{1,0:T(8,128)(2,1)} %bitcast.54, f32[1024,768]{1,0:T(8,128)} %get-tuple-element.81.gm_ref, ...), custom_call_target="tpu_custom_call" | custom-call | flops 7247757312 | bytes 25165824 | tf_op jit(solution)/shard_map/pallas_call | solution.py:744
  269.0 109.4 %shard_map.183 = (bf16[4,256,768]{2,1,0:T(8,128)(2,1)}, f32[24,2304]{1,0:T(8,128)}, f32[8,128]{1,0:T(8,128)}, f32[24,768]{1,0:T(8,128)}, f32[24,3072]{1,0:T(8,128)}, /*index=5*/f32[96,768]{1,0:T(8,128)}) custom-call(bf16[4,256,768]{2,1,0:T(8,128)(2,1)} %bitcast.61, bf16[8,96,2304]{2,1,0:T(8,128)(2,1)} %bitcast.57, f32[8,32,128]{2,1,0:T(8,128)} %bitcast.63, ...), custom_call_target="tpu_custom_call" | custom-call | tf_op jit(solution)/shard_map/pallas_call | solution.py:898
  378.4 1.3 slice_bitcast_fusion.5
  379.7 1.3 slice_bitcast_fusion.6
  381.0 3.1 reshape.461
  384.1 1.4 copy.71
  386.0 1.1 copy.90
  388.4 0.7 copy.93
  389.1 0.7 copy.94
  (75 shorter events, 10.2 us)
Async XLA Ops:
  80.3 6.2 %copy-start.4 = (bf16[4,256,768]{2,1,0:T(8,128)(2,1)S(1)}, bf16[4,256,768]{2,1,0:T(8,128)(2,1)}, u32[]{:S(2)}) copy-start(bf16[4,256,768]{2,1,0:T(8,128)(2,1)} %get-tuple-element.66) | copy-start | bytes 4718596
  80.3 56.3 %all-to-all-start = ((bf16[4,256,768]{2,1,0:T(8,128)(2,1)}), bf16[4,256,768]{2,1,0:T(8,128)(2,1)}, u32[]{:S(2)}, u32[]{:S(2)}) async-start(bf16[4,256,768]{2,1,0:T(8,128)(2,1)} %broadcast_multiply_fusion), calls=%async_computation | async-start | bytes 3145728 | tf_op jit(solution)/shard_map/all_to_all | solution.py:952
  90.0 3.6 copy-start.13
  90.3 3.5 copy-start.6
  98.4 4.2 %copy-start.5 = (bf16[4,256,768]{2,1,0:T(8,128)(2,1)S(1)}, bf16[4,256,768]{2,1,0:T(8,128)(2,1)}, u32[]{:S(2)}) copy-start(bf16[4,256,768]{2,1,0:T(8,128)(2,1)} %get-tuple-element.66) | copy-start | bytes 4718596
  98.4 4.6 %copy-start.15 = (bf16[32,24,2304]{2,1,0:T(8,128)(2,1)S(1)}, bf16[32,24,2304]{2,1,0:T(8,128)(2,1)}, u32[]{:S(2)}) copy-start(bf16[32,24,2304]{2,1,0:T(8,128)(2,1)} %get-tuple-element.68) | copy-start | bytes 10616836
  135.5 1.1 copy-start.3
  201.4 179.5 %all-to-all-start.1 = ((bf16[4,2,98304]{2,1,0:T(2,128)(2,1)}), bf16[4,2,98304]{2,1,0:T(2,128)(2,1)}, u32[]{:S(2)}, u32[]{:S(2)}) async-start(bf16[4,2,98304]{2,1,0:T(2,128)(2,1)} %reshape.460), calls=%async_computation.1 | async-start | bytes 3145728 | tf_op jit(solution)/shard_map/all_to_all | solution.py:965
  206.5 39.9 %copy-start.7 = (s32[128,384]{1,0:T(8,128)S(1)}, s32[128,384]{1,0:T(8,128)}, u32[]{:S(2)}) copy-start(s32[128,384]{1,0:T(8,128)} %copy-done.6) | copy-start | bytes 589828
  242.6 1.1 copy-start
  243.8 1.1 copy-start.1
  244.9 1.1 copy-start.2
  252.7 15.4 %copy-start.14 = (f32[1,768]{1,0:T(1,128)S(1)}, f32[1,768]{1,0:T(1,128)}, u32[]{:S(2)}) copy-start(f32[1,768]{1,0:T(1,128)} %get-tuple-element.85) | copy-start | bytes 9220
  384.0 1.9 copy-start.8
  385.5 1.6 copy-start.11
  385.5 2.3 copy-start.12
  385.5 3.0 copy-start.10
  385.5 3.7 copy-start.9
